TPU v7x, 32 devices: a whole 2x2x4 slice. The times are simulated.
32 devices in a mesh: fsdp: 4 (over y, x), ctx: 4 (over z), tp: 2 (over core).
Axes of the slice: x: 2, y: 2, z: 4, core: 2. Of those that a mesh axis runs over, the one named last changes fastest.
Arguments:
- tokens: bfloat16 [16384, 1152], P(('fsdp', 'ctx')), may hold values from -6 to 6
- positions: int32 [16384], P(('fsdp', 'ctx')), may hold values from 0 to 4095, as said below
- query_weight: bfloat16 [1152, 1024], P('fsdp', 'tp'), may hold values from -0.1875 to 0.1875
- keyvalue_weight: bfloat16 [1152, 512], P('fsdp'), may hold values from -0.1875 to 0.1875
- output_weight: bfloat16 [1024, 1152], P('tp', 'fsdp'), may hold values from -0.1875 to 0.1875
- gate_weight: bfloat16 [1152, 6912], P('fsdp', 'tp'), may hold values from -0.1875 to 0.1875
- up_weight: bfloat16 [1152, 6912], P('fsdp', 'tp'), may hold values from -0.1875 to 0.1875
- down_weight: bfloat16 [6912, 1152], P('tp', 'fsdp'), may hold values from -0.078125 to 0.078125
- input_gain: bfloat16 [1152], P('fsdp'), may hold values from -0.5 to 0.5
- query_gain: bfloat16 [256], P('fsdp'), may hold values from -0.5 to 0.5
- key_gain: bfloat16 [256], P('fsdp'), may hold values from -0.5 to 0.5
- attention_gain: bfloat16 [1152], P('fsdp'), may hold values from -0.5 to 0.5
- middle_gain: bfloat16 [1152], P('fsdp'), may hold values from -0.5 to 0.5
- final_gain: bfloat16 [1152], P('fsdp'), may hold values from -0.5 to 0.5
- cotangent: bfloat16 [16384, 1152], P(('fsdp', 'ctx')), may hold values from -6 to 6
Outputs:
- layer_out: bfloat16 [16384, 1152], P(('fsdp', 'ctx'))
- tokens_grad: bfloat16 [16384, 1152], P(('fsdp', 'ctx'))
- query_weight_grad: float32 [1152, 1024], P('fsdp', 'tp')
- keyvalue_weight_grad: float32 [1152, 512], P('fsdp')
- output_weight_grad: float32 [1024, 1152], P('tp', 'fsdp')
- gate_weight_grad: float32 [1152, 6912], P('fsdp', 'tp')
- up_weight_grad: float32 [1152, 6912], P('fsdp', 'tp')
- down_weight_grad: float32 [6912, 1152], P('tp', 'fsdp')
- input_gain_grad: float32 [1152], P('fsdp')
- query_gain_grad: float32 [256], P('fsdp')
- key_gain_grad: float32 [256], P('fsdp')
- attention_gain_grad: float32 [1152], P('fsdp')
- middle_gain_grad: float32 [1152], P('fsdp')
- final_gain_grad: float32 [1152], P('fsdp')
Inputs may be any that keep to these rules, and one draw needn't show every extreme that they name: Each run of 4096 tokens of one fsdp index holds whole sequences; within a sequence positions run 0, 1, 2 and so on; every sequence has 1024 tokens or more; some such run holds one sequence only.
All inputs are finite; a program needn't handle non-finite values.
Results may differ from a plain program's by a relative error of at most 0.023.
Values may be sent and summed in bfloat16 or wider, within the bound.
No kernel may reach another device: no remote copies, remote signals or barrier semaphores. Data moves between devices by JAX's collectives and lax.ppermute only.
A program may use at most 256 MiB of HBM per device.

v0:
```python
from functools import partial

import jax
import jax.numpy as jnp
from jax import lax
from jax.sharding import PartitionSpec as P

WINDOW = 512


EPS = 1e-06
SCALE = 0.0625
NEG = -1e30


def passed_along(value, axis, steps):
    count = lax.axis_size(axis)
    first, last = (max(0, -steps), min(count, count - steps))
    return lax.ppermute(value, axis, [(source, source + steps) for source in range(first, last)])


def normalize(values):
    inverse = lax.rsqrt(jnp.mean(values * values, axis=-1, keepdims=True) + EPS)
    return (values * inverse, inverse)


def norm_back(gradient, normed, inverse):
    return inverse * (gradient - normed * jnp.mean(gradient * normed, axis=-1, keepdims=True))


def rotate(values, cosine_table, sine_table):
    half_width = values.shape[-1] // 2
    front_half = values[..., :half_width]
    back_half = values[..., half_width:]
    return jnp.concatenate(
        [
            front_half * cosine_table - back_half * sine_table,
            back_half * cosine_table + front_half * sine_table,
        ],
        axis=-1,
    )


def rotary(positions, head_width):
    half_width = head_width // 2
    frequency = 10000.0 ** (-(2.0 * jnp.arange(half_width).astype(jnp.float32)) / head_width)
    angles = positions.astype(jnp.float32)[:, None] * frequency[None, :]
    return (jnp.cos(angles), jnp.sin(angles))


def product(left, right):
    return jnp.dot(left, right, preferred_element_type=jnp.float32)


def inner_rows(left, right):
    return lax.dot_general(
        left, right, (((0,), (0,)), ((), ())), preferred_element_type=jnp.float32
    )


def inner_cols(left, right):
    return lax.dot_general(
        left, right, (((1,), (1,)), ((), ())), preferred_element_type=jnp.float32
    )


def shards(
    tokens,
    positions,
    query_weight,
    keyvalue_weight,
    output_weight,
    gate_weight,
    up_weight,
    down_weight,
    input_gain,
    query_gain,
    key_gain,
    attention_gain,
    middle_gain,
    final_gain,
    cotangent,
):
    query_full, keyvalue_full, output_full, input_scale, query_scale, key_scale, attention_scale = (
        lax.all_gather(query_weight, "fsdp", axis=0, tiled=True),
        lax.all_gather(keyvalue_weight, "fsdp", axis=0, tiled=True),
        lax.all_gather(output_weight, "fsdp", axis=1, tiled=True),
        lax.all_gather(input_gain, "fsdp", axis=0, tiled=True),
        lax.all_gather(query_gain, "fsdp", axis=0, tiled=True),
        lax.all_gather(key_gain, "fsdp", axis=0, tiled=True),
        lax.all_gather(attention_gain, "fsdp", axis=0, tiled=True),
    )
    gate_full, up_full, down_full, middle_scale, final_scale = (
        lax.all_gather(gate_weight, "fsdp", axis=0, tiled=True),
        lax.all_gather(up_weight, "fsdp", axis=0, tiled=True),
        lax.all_gather(down_weight, "fsdp", axis=1, tiled=True),
        lax.all_gather(middle_gain, "fsdp", axis=0, tiled=True),
        lax.all_gather(final_gain, "fsdp", axis=0, tiled=True),
    )
    input_factor = 1.0 + input_scale.astype(jnp.float32)
    query_factor = 1.0 + query_scale.astype(jnp.float32)
    key_factor = 1.0 + key_scale.astype(jnp.float32)
    attention_factor = 1.0 + attention_scale.astype(jnp.float32)
    middle_factor = 1.0 + middle_scale.astype(jnp.float32)
    final_factor = 1.0 + final_scale.astype(jnp.float32)
    tok_rows = tokens.shape[0]
    head_width = query_scale.shape[0]
    local_heads = query_full.shape[1] // head_width
    rim_rows = WINDOW - 1
    block_rows = min(512, tok_rows)
    block_count = tok_rows // block_rows
    slab_rows = block_rows + rim_rows
    inputs = tokens.astype(jnp.float32)
    normed_in, inverse_in = normalize(inputs)
    hidden = (normed_in * input_factor).astype(jnp.bfloat16)
    query_raw = product(hidden, query_full).reshape(tok_rows, local_heads, head_width)
    keyvalue_raw = product(hidden, keyvalue_full)
    cosine_table, sine_table = rotary(positions, head_width)
    cosine_heads = cosine_table[:, None, :]
    sine_heads = sine_table[:, None, :]
    query_normed, query_inverse = normalize(query_raw)
    query_rot = rotate(query_normed * query_factor, cosine_heads, sine_heads).astype(jnp.bfloat16)
    key_normed, key_inverse = normalize(keyvalue_raw[:, :head_width])
    key_rot = rotate(key_normed * key_factor, cosine_table, sine_table)
    keyvalue = jnp.concatenate([key_rot, keyvalue_raw[:, head_width:]], axis=1).astype(jnp.bfloat16)
    earlier = passed_along(keyvalue[tok_rows - rim_rows :], "ctx", 1)
    keyvalue_ext = jnp.concatenate([earlier, keyvalue], axis=0)
    lag_table = (
        lax.broadcasted_iota(jnp.int32, (block_rows, slab_rows), 0)
        - lax.broadcasted_iota(jnp.int32, (block_rows, slab_rows), 1)
        + rim_rows
    )
    block_starts = jnp.arange(block_count, dtype=jnp.int32) * block_rows

    def scores_for(row_start):
        query_block = lax.dynamic_slice_in_dim(query_rot, row_start, block_rows, 0)
        key_slab = lax.dynamic_slice_in_dim(keyvalue_ext, row_start, slab_rows, 0)
        key_block = key_slab[:, :head_width]
        value_block = key_slab[:, head_width:]
        reach = jnp.minimum(
            lax.dynamic_slice_in_dim(positions, row_start, block_rows, 0), rim_rows
        )[:, None]
        allowed = (lag_table >= 0) & (lag_table <= reach)
        scores = (
            jnp.einsum("rhd,sd->hrs", query_block, key_block, preferred_element_type=jnp.float32)
            * SCALE
        )
        return (query_block, key_block, value_block, jnp.where(allowed[None], scores, NEG))

    def forward_block(row_start):
        query_block, key_block, value_block, scores = scores_for(row_start)
        highest = jnp.max(scores, axis=-1, keepdims=True)
        shifted = jnp.exp(scores - highest)
        totals = jnp.sum(shifted, axis=-1, keepdims=True)
        weights = (shifted / totals).astype(jnp.bfloat16)
        mixed = jnp.einsum("hrs,sd->rhd", weights, value_block, preferred_element_type=jnp.float32)
        return (mixed, (highest + jnp.log(totals))[..., 0])

    mixed_blocks, logsum_blocks = lax.map(forward_block, block_starts)
    attended = mixed_blocks.reshape(tok_rows, local_heads * head_width).astype(jnp.bfloat16)
    branch = lax.psum(product(attended, output_full), "tp")
    branch_normed, branch_inverse = normalize(branch)
    residual = inputs + branch_normed * attention_factor
    middle_normed, middle_inverse = normalize(residual)
    hidden_ffn = (middle_normed * middle_factor).astype(jnp.bfloat16)
    gate_value = product(hidden_ffn, gate_full)
    up_value = product(hidden_ffn, up_full)
    activated, gelu_pull = jax.vjp(partial(jax.nn.gelu, approximate=True), gate_value)
    feed = (activated * up_value).astype(jnp.bfloat16)
    outcome = lax.psum(product(feed, down_full).astype(jnp.bfloat16), "tp").astype(jnp.float32)
    outcome_normed, outcome_inverse = normalize(outcome)
    layer_out = (residual + outcome_normed * final_factor).astype(jnp.bfloat16)
    upstream = cotangent.astype(jnp.float32)
    final_gain_grad = jnp.sum(upstream * outcome_normed, axis=0)
    outcome_grad = norm_back(upstream * final_factor, outcome_normed, outcome_inverse).astype(
        jnp.bfloat16
    )
    feed_grad = inner_cols(outcome_grad, down_full)
    down_weight_grad = inner_rows(feed, outcome_grad)
    gate_grad = gelu_pull(feed_grad * up_value)[0].astype(jnp.bfloat16)
    up_grad = (feed_grad * activated).astype(jnp.bfloat16)
    gate_weight_grad = inner_rows(hidden_ffn, gate_grad)
    up_weight_grad = inner_rows(hidden_ffn, up_grad)
    hidden_ffn_grad = lax.psum(
        (inner_cols(gate_grad, gate_full) + inner_cols(up_grad, up_full)).astype(jnp.bfloat16), "tp"
    ).astype(jnp.float32)
    middle_gain_grad = jnp.sum(hidden_ffn_grad * middle_normed, axis=0)
    residual_grad = upstream + norm_back(
        hidden_ffn_grad * middle_factor, middle_normed, middle_inverse
    )
    attention_gain_grad = jnp.sum(residual_grad * branch_normed, axis=0)
    branch_grad = norm_back(residual_grad * attention_factor, branch_normed, branch_inverse).astype(
        jnp.bfloat16
    )
    output_weight_grad = inner_rows(attended, branch_grad)
    attended_grad = inner_cols(branch_grad, output_full).astype(jnp.bfloat16)
    attended_heads = attended_grad.reshape(tok_rows, local_heads, head_width)

    def backward_block(slab_grad, block_args):
        row_start, logsum = block_args
        query_block, key_block, value_block, scores = scores_for(row_start)
        weights = jnp.exp(scores - logsum[..., None])
        upper_grad = lax.dynamic_slice_in_dim(attended_heads, row_start, block_rows, 0)
        weight_grad = jnp.einsum(
            "rhd,sd->hrs", upper_grad, value_block, preferred_element_type=jnp.float32
        )
        centred = jnp.sum(weights * weight_grad, axis=-1, keepdims=True)
        score_grad = (weights * (weight_grad - centred)).astype(jnp.bfloat16)
        query_part = (
            jnp.einsum("hrs,sd->rhd", score_grad, key_block, preferred_element_type=jnp.float32)
            * SCALE
        )
        key_part = (
            jnp.einsum("hrs,rhd->sd", score_grad, query_block, preferred_element_type=jnp.float32)
            * SCALE
        )
        value_part = jnp.einsum(
            "hrs,rhd->sd",
            weights.astype(jnp.bfloat16),
            upper_grad,
            preferred_element_type=jnp.float32,
        )
        current = lax.dynamic_slice_in_dim(slab_grad, row_start, slab_rows, 0)
        updated = current + jnp.concatenate([key_part, value_part], axis=1)
        return (lax.dynamic_update_slice_in_dim(slab_grad, updated, row_start, 0), query_part)

    slab_zero = jnp.zeros((tok_rows + rim_rows, 2 * head_width), jnp.float32)
    extended_grad, query_parts = lax.scan(backward_block, slab_zero, (block_starts, logsum_blocks))
    query_turned = query_parts.reshape(tok_rows, local_heads, head_width)
    query_unturned = rotate(query_turned, cosine_heads, -sine_heads)
    query_gain_part = jnp.sum(query_unturned * query_normed, axis=(0, 1))
    extended_grad, query_gain_grad = (
        lax.psum(extended_grad.astype(jnp.bfloat16), "tp").astype(jnp.float32),
        lax.psum(query_gain_part.astype(jnp.bfloat16), "tp").astype(jnp.float32),
    )
    returned = passed_along(extended_grad[:rim_rows].astype(jnp.bfloat16), "ctx", -1).astype(
        jnp.float32
    )
    keyvalue_grad = extended_grad[rim_rows:].at[tok_rows - rim_rows :].add(returned)
    key_unturned = rotate(keyvalue_grad[:, :head_width], cosine_table, -sine_table)
    key_gain_grad = jnp.sum(key_unturned * key_normed, axis=0)
    key_raw_grad = norm_back(key_unturned * key_factor, key_normed, key_inverse)
    keyvalue_raw_grad = jnp.concatenate(
        [key_raw_grad, keyvalue_grad[:, head_width:]], axis=1
    ).astype(jnp.bfloat16)
    query_raw_grad = (
        norm_back(query_unturned * query_factor, query_normed, query_inverse)
        .reshape(tok_rows, local_heads * head_width)
        .astype(jnp.bfloat16)
    )
    hidden_grad = lax.psum(
        inner_cols(query_raw_grad, query_full).astype(jnp.bfloat16), "tp"
    ).astype(jnp.float32) + inner_cols(keyvalue_raw_grad, keyvalue_full)
    query_weight_grad = inner_rows(hidden, query_raw_grad)
    keyvalue_weight_grad = inner_rows(hidden, keyvalue_raw_grad)
    input_gain_grad = jnp.sum(hidden_grad * normed_in, axis=0)
    tokens_grad = (
        residual_grad + norm_back(hidden_grad * input_factor, normed_in, inverse_in)
    ).astype(jnp.bfloat16)
    (
        query_share,
        keyvalue_share,
        output_share,
        gate_share,
        up_share,
        down_share,
        input_share,
        query_gshare,
        key_share,
        attention_share,
        middle_share,
        final_share,
    ) = (
        lax.psum_scatter(
            query_weight_grad.astype(jnp.bfloat16), "fsdp", scatter_dimension=0, tiled=True
        ).astype(jnp.float32),
        lax.psum_scatter(
            keyvalue_weight_grad.astype(jnp.bfloat16), "fsdp", scatter_dimension=0, tiled=True
        ).astype(jnp.float32),
        lax.psum_scatter(
            output_weight_grad.astype(jnp.bfloat16), "fsdp", scatter_dimension=1, tiled=True
        ).astype(jnp.float32),
        lax.psum_scatter(
            gate_weight_grad.astype(jnp.bfloat16), "fsdp", scatter_dimension=0, tiled=True
        ).astype(jnp.float32),
        lax.psum_scatter(
            up_weight_grad.astype(jnp.bfloat16), "fsdp", scatter_dimension=0, tiled=True
        ).astype(jnp.float32),
        lax.psum_scatter(
            down_weight_grad.astype(jnp.bfloat16), "fsdp", scatter_dimension=1, tiled=True
        ).astype(jnp.float32),
        lax.psum_scatter(
            input_gain_grad.astype(jnp.bfloat16), "fsdp", scatter_dimension=0, tiled=True
        ).astype(jnp.float32),
        lax.psum_scatter(
            query_gain_grad.astype(jnp.bfloat16), "fsdp", scatter_dimension=0, tiled=True
        ).astype(jnp.float32),
        lax.psum_scatter(
            key_gain_grad.astype(jnp.bfloat16), "fsdp", scatter_dimension=0, tiled=True
        ).astype(jnp.float32),
        lax.psum_scatter(
            attention_gain_grad.astype(jnp.bfloat16), "fsdp", scatter_dimension=0, tiled=True
        ).astype(jnp.float32),
        lax.psum_scatter(
            middle_gain_grad.astype(jnp.bfloat16), "fsdp", scatter_dimension=0, tiled=True
        ).astype(jnp.float32),
        lax.psum_scatter(
            final_gain_grad.astype(jnp.bfloat16), "fsdp", scatter_dimension=0, tiled=True
        ).astype(jnp.float32),
    )
    shares = (
        lax.psum(query_share.astype(jnp.bfloat16), "ctx").astype(jnp.float32),
        lax.psum(keyvalue_share.astype(jnp.bfloat16), "ctx").astype(jnp.float32),
        lax.psum(output_share.astype(jnp.bfloat16), "ctx").astype(jnp.float32),
        lax.psum(gate_share.astype(jnp.bfloat16), "ctx").astype(jnp.float32),
        lax.psum(up_share.astype(jnp.bfloat16), "ctx").astype(jnp.float32),
        lax.psum(down_share.astype(jnp.bfloat16), "ctx").astype(jnp.float32),
        lax.psum(input_share.astype(jnp.bfloat16), "ctx").astype(jnp.float32),
        lax.psum(query_gshare.astype(jnp.bfloat16), "ctx").astype(jnp.float32),
        lax.psum(key_share.astype(jnp.bfloat16), "ctx").astype(jnp.float32),
        lax.psum(attention_share.astype(jnp.bfloat16), "ctx").astype(jnp.float32),
        lax.psum(middle_share.astype(jnp.bfloat16), "ctx").astype(jnp.float32),
        lax.psum(final_share.astype(jnp.bfloat16), "ctx").astype(jnp.float32),
    )
    return (
        layer_out,
        tokens_grad,
        shares[0],
        shares[1],
        shares[2],
        shares[3],
        shares[4],
        shares[5],
        shares[6],
        shares[7],
        shares[8],
        shares[9],
        shares[10],
        shares[11],
    )


def solution(mesh):
    placed = (
        P(("fsdp", "ctx"), None),
        P(("fsdp", "ctx")),
        P("fsdp", "tp"),
        P("fsdp", None),
        P("tp", "fsdp"),
        P("fsdp", "tp"),
        P("fsdp", "tp"),
        P("tp", "fsdp"),
        P("fsdp"),
        P("fsdp"),
        P("fsdp"),
        P("fsdp"),
        P("fsdp"),
        P("fsdp"),
        P(("fsdp", "ctx"), None),
    )
    return jax.shard_map(
        shards,
        mesh=mesh,
        in_specs=placed,
        out_specs=(
            P(("fsdp", "ctx"), None),
            P(("fsdp", "ctx"), None),
            P("fsdp", "tp"),
            P("fsdp", None),
            P("tp", "fsdp"),
            P("fsdp", "tp"),
            P("fsdp", "tp"),
            P("tp", "fsdp"),
            P("fsdp"),
            P("fsdp"),
            P("fsdp"),
            P("fsdp"),
            P("fsdp"),
            P("fsdp"),
        ),
        check_vma=False,
    )
```

profile of v0, /device:TPU:0, one launch (start us, length us, event | category | flops | bytes accessed | tf_op | source)
XLA Modules:
  0.0 1305.8 jit_solution(9487846979598609221)
XLA Ops:
  17.3 18.1 %all-reduce.15 = (bf16[1152]{0:T(1024)(128)(2,1)S(1)}, bf16[256]{0:T(256)(128)(2,1)S(1)}, bf16[256]{0:T(256)(128)(2,1)S(1)}, bf16[1152]{0:T(1024)(128)(2,1)S(1)}...) all-reduce(bf16[1152]{0:T(1024)(128)(2,1)S(1)} %dynamic-update-slic, ...), channel_id=1, replica_groups=mesh['fsdp'=4,'ctx'=4,'tp'=2] {'fsdp'}, use_global_device_ids=true, to_apply=%add | all-reduce | flops 5120 | bytes 20480
  45.6 24.4 %all-gather.9.cloned.1.call-done = bf16[1152,512]{1,0:T(8,128)(2,1)} async-done(((bf16[288,512]{1,0:T(8,128)(2,1)}), bf16[1152,512]{1,0:T(8,128)(2,1)}) %all-gather.9.cloned.1.call-update) | async-done | bytes 1179664 | tf_op jit(solution)/shard_map/all_gather | solution.py:85
  103.8 29.2 %while.29 = (s32[]{:T(128)}, bf16[2,512,2,256]{1,3,2,0:T(8,128)(2,1)}, f32[2,2,512]{2,1,0:T(2,128)S(1)}, s32[2]{0:T(128)S(1)}, bf16[1535,512]{1,0:T(8,128)(2,1)}...) while((s32[]{:T(128)}, ...), condition=%wide.region_6.7_spmd.clone.clone, body=%wide.region_3.6_spmd.clone.clone.sunk | while | flops 1087882240 | bytes 34091772 | solution.py:159
  146.9 27.5 %all-reduce.23.cloned.1.call-done = f32[1024,1152]{1,0:T(8,128)} async-done(((f32[1024,1152]{1,0:T(8,128)}), f32[1024,1152]{1,0:T(8,128)}) %all-reduce.23.cloned.1.call-update) | async-done | bytes 4718608 | tf_op jit(solution)/shard_map/psum | solution.py:161
  182.1 79.2 %all-gather.13.cloned.1.call-done = bf16[1152,3456]{1,0:T(8,128)(2,1)} async-done(((bf16[288,3456]{1,0:T(8,128)(2,1)}), bf16[1152,3456]{1,0:T(8,128)(2,1)}) %all-gather.13.cloned.1.call-update) | async-done | bytes 7962640 | tf_op jit(solution)/shard_map/all_gather | solution.py:94
  261.3 14.8 %fusion.115 = f32[1024,3456]{1,0:T(8,128)} fusion(bf16[1024,1152]{1,0:T(8,128)(2,1)S(1)} %multiply_convert_fusion.3, bf16[1152,3456]{1,0:T(8,128)(2,1)} %all-gather.13.cloned.1.call-done), kind=kOutput, calls=%fused_computation.206 | convolution fusion | flops 8153726976 | bytes 24477696 | tf_op jit(solution)/shard_map/dot_general | solution.py:52
  276.0 70.9 %all-gather.15.cloned.1.call-done = bf16[1152,3456]{1,0:T(8,128)(2,1)} async-done(((bf16[288,3456]{1,0:T(8,128)(2,1)}), bf16[1152,3456]{1,0:T(8,128)(2,1)}) %all-gather.15.cloned.1.call-update) | async-done | bytes 7962640 | tf_op jit(solution)/shard_map/all_gather | solution.py:95
  346.9 20.6 %multiply_convert_fusion.1 = (bf16[1024,3456]{1,0:T(8,128)(2,1)}, f32[1024,3456]{1,0:T(8,128)}) fusion(f32[1024,3456]{1,0:T(8,128)} %fusion.115, bf16[1024,1152]{1,0:T(8,128)(2,1)S(1)} %multiply_convert_fusion.3, bf16[1152,3456]{1,0:T(8,128)(2,1)} %all-gather.15.cloned.1.call-done), kind=kOutput, calls=%fused_computation.78 | convolution fusion | flops 8189116416 | bytes 45711360 | tf_op jit(solution)/shard_map/dot_general | solution.py:52
  367.6 65.2 %all-gather.17.cloned.1.call-done = bf16[3456,1152]{0,1:T(8,128)(2,1)} async-done(((bf16[3456,288]{0,1:T(8,128)(2,1)}), bf16[3456,1152]{0,1:T(8,128)(2,1)}) %all-gather.17.cloned.1.call-update) | async-done | bytes 7962640 | tf_op jit(solution)/shard_map/all_gather | solution.py:96
  432.8 15.0 %convolution_convert_fusion.3 = bf16[1024,1152]{1,0:T(8,128)(2,1)} fusion(bf16[1024,3456]{1,0:T(8,128)(2,1)} %get-tuple-element.375, bf16[3456,1152]{0,1:T(8,128)(2,1)} %all-gather.17.cloned.1.call-done), kind=kOutput, calls=%fused_computation.126 | convolution fusion | flops 8154906624 | bytes 17399808 | tf_op jit(solution)/shard_map/dot_general | solution.py:52
  447.9 21.8 %all-reduce.25.cloned.1.call-done = bf16[1024,1152]{1,0:T(8,128)(2,1)} async-done(((bf16[1024,1152]{1,0:T(8,128)(2,1)}), bf16[1024,1152]{1,0:T(8,128)(2,1)}) %all-reduce.25.cloned.1.call-update) | async-done | bytes 2359312 | tf_op jit(solution)/shard_map/psum | solution.py:170
  476.6 27.4 %multiply_convert_fusion = (bf16[1024,3456]{1,0:T(8,128)(2,1)}, bf16[1024,3456]{1,0:T(8,128)(2,1)}) fusion(f32[1024,3456]{1,0:T(8,128)} %fusion.115, f32[1024,3456]{1,0:T(8,128)} %get-tuple-element.376, bf16[3456,1152]{0,1:T(8,128)(2,1)} %all-gather.17.cloned.1.call-done, bf16[1024,1152]{1,0:T(8,128)(2,1)} %param.35, bf16[1024,1152]{1,0:T(8,128)(2,1)S(1)} %copy-done.7, ...), kind=kOutput, calls=%fused_computation.77 | convolution fusion | flops 8248098816 | bytes 55161344 | tf_op jit(solution)/shard_map/dot_general | solution.py:62
  503.9 15.7 %fusion.116 = f32[1024,1152]{1,0:T(8,128)} fusion(bf16[1024,3456]{1,0:T(8,128)(2,1)} %get-tuple-element.352, bf16[1152,3456]{1,0:T(8,128)(2,1)} %all-gather.13.cloned.1.call-done), kind=kOutput, calls=%fused_computation.207 | convolution fusion | flops 8153726976 | bytes 19759104 | tf_op jit(solution)/shard_map/dot_general | solution.py:62
  519.6 14.9 %add_convert_fusion = bf16[1024,1152]{1,0:T(8,128)(2,1)} fusion(f32[1024,1152]{1,0:T(8,128)} %fusion.116, bf16[1024,3456]{1,0:T(8,128)(2,1)S(1)} %copy-done.66, bf16[1152,3456]{1,0:T(8,128)(2,1)} %all-gather.15.cloned.1.call-done), kind=kOutput, calls=%fused_computation.122 | convolution fusion | flops 8156086272 | bytes 22118400 | tf_op jit(solution)/shard_map/dot_general | solution.py:62
  535.9 21.8 %all-reduce.27.cloned.1.call-done = bf16[1024,1152]{1,0:T(8,128)(2,1)} async-done(((bf16[1024,1152]{1,0:T(8,128)(2,1)}), bf16[1024,1152]{1,0:T(8,128)(2,1)}) %all-reduce.27.cloned.1.call-update) | async-done | bytes 2359312 | tf_op jit(solution)/shard_map/psum | solution.py:184
  577.7 68.5 %while.30 = (s32[]{:T(128)}, f32[1535,512]{0,1:T(8,128)}, f32[2,512,2,256]{3,1,0,2:T(8,128)}, s32[2]{0:T(128)S(1)}, s32[1024]{0:T(1024)S(1)}, /*index=5*/bf16[15...) while((s32[]{:T(128)}, f32[1535,512]{0,1:T(8,128)}, ...), condition=%wide.region_18.19_spmd.clone.clone, body=%wide.region_16.18_spmd.clone.clone.sunk | while | flops 2701636352 | bytes 84380472 | solution.py:228
  669.9 17.4 %all-reduce.31.cloned.1.call-done = (bf16[1024,1152]{1,0:T(8,128)(2,1)}, bf16[1535,512]{0,1:T(8,128)(2,1)}) async-done(((bf16[1024,1152]{1,0:T(8,128)(2,1)}, bf16[1535,512]{0,1:T(8,128)(2,1)}), (bf16[1024,1152]{1,0:T(8,128)(2,1)}, bf16[1535,512]{0,1:T(8,128)(2,1)})) %all-reduce.31.cloned.1.call-update) | async-done | bytes 3931152 | tf_op jit(solution)/shard_map/psum | solution.py:251
  719.2 14.6 %convolution_convert_fusion = bf16[3456,1152]{0,1:T(8,128)(2,1)} fusion(bf16[1024,3456]{1,0:T(8,128)(2,1)} %get-tuple-element.375, bf16[1024,1152]{1,0:T(8,128)(2,1)} %param.35, bf16[1024,1152]{1,0:T(8,128)(2,1)S(1)} %copy-done.8, f32[1024]{0:T(1024)S(1)} %copy-done.59, f32[1152]{0:T(1024)S(1)} %convert_add_fusion.2, f32[1024]{0:T(1024)S(1)} %add_rsqrt_fusion.1), kind=kOutput, calls=%fused_computation.67 | convolution fusion | flops 8167145472 | bytes 19771904 | tf_op jit(solution)/shard_map/dot_general | solution.py:56
  763.6 20.9 %reduce-scatter.9.cloned.1.call-done = bf16[288,512]{1,0:T(8,128)(2,1)} async-done(((bf16[1152,512]{1,0:T(8,128)(2,1)}), bf16[288,512]{1,0:T(8,128)(2,1)}) %reduce-scatter.9.cloned.1.call-update) | async-done | bytes 294928 | tf_op jit(solution)/shard_map/reduce_scatter | solution.py:277
  784.6 86.2 %reduce-scatter.17.cloned.1.call-done = bf16[3456,288]{0,1:T(8,128)(2,1)} async-done(((bf16[3456,1152]{0,1:T(8,128)(2,1)}), bf16[3456,288]{0,1:T(8,128)(2,1)}) %reduce-scatter.17.cloned.1.call-update) | async-done | bytes 1990672 | tf_op jit(solution)/shard_map/reduce_scatter | solution.py:289
  870.8 86.2 %reduce-scatter.13.cloned.1.call-done = bf16[288,3456]{1,0:T(8,128)(2,1)} async-done(((bf16[1152,3456]{1,0:T(8,128)(2,1)}), bf16[288,3456]{1,0:T(8,128)(2,1)}) %reduce-scatter.13.cloned.1.call-update) | async-done | bytes 1990672 | tf_op jit(solution)/shard_map/reduce_scatter | solution.py:283
  957.0 86.2 %reduce-scatter.15.cloned.1.call-done = bf16[288,3456]{1,0:T(8,128)(2,1)} async-done(((bf16[1152,3456]{1,0:T(8,128)(2,1)}), bf16[288,3456]{1,0:T(8,128)(2,1)}) %reduce-scatter.15.cloned.1.call-update) | async-done | bytes 1990672 | tf_op jit(solution)/shard_map/reduce_scatter | solution.py:286
  1050.6 15.4 %all-reduce.14 = (bf16[1152]{0:T(1024)(128)(2,1)S(1)}, bf16[256]{0:T(256)(128)(2,1)S(1)}, bf16[256]{0:T(256)(128)(2,1)S(1)}, bf16[1152]{0:T(1024)(128)(2,1)S(1)}...) all-reduce(bf16[1152]{0:T(1024)(128)(2,1)S(1)} %get-tuple-element.2, ...), channel_id=8, replica_groups=mesh['fsdp'=4,'ctx'=4,'tp'=2] {'fsdp'}, use_global_device_ids=true, to_apply=%region_37.38.clone | all-reduce | flops 5120 | bytes 20480
  1090.4 197.5 %all-reduce.29.cloned.1.call-done = (bf16[288,512]{1,0:T(8,128)(2,1)}, bf16[288,512]{1,0:T(8,128)(2,1)}, bf16[512,288]{0,1:T(8,128)(2,1)}, bf16[288,3456]{1,0:T(...) async-done(((bf16[288,512]{1,0:T(8,128)(2,1)}, bf16[288,512]{1,0:T(8,128)(2,1)}, bf16[512,288]{0,1:T(8,128)(2,1)}, bf16[288,3456]{1,0:T(8,128)(2,1)}, ...) | async-done | bytes 6856720 | tf_op jit(solution)/shard_map/psum | solution.py:312
  (342 shorter events, 313.3 us)
Async XLA Ops:
  7.2 33.3 %all-gather.7.cloned.1.call-start = ((), (), s32[]{:S(2)}) async-start(), calls=%async_computation.6 | async-start | bytes 1474560 | tf_op jit(solution)/shard_map/all_gather | solution.py:86
  7.9 62.0 %all-gather.9.cloned.1.call-start = ((), (), s32[]{:S(2)}) async-start(), calls=%async_computation.7 | async-start | bytes 1474560 | tf_op jit(solution)/shard_map/all_gather | solution.py:85
  8.7 130.4 %all-gather.11.cloned.1.call-start = ((), (), s32[]{:S(2)}) async-start(), calls=%async_computation.8 | async-start | bytes 1474560 | tf_op jit(solution)/shard_map/all_gather | solution.py:87
  9.4 165.0 %all-reduce.23.cloned.1.call-start = ((), (), s32[]{:S(2)}) async-start(), calls=%async_computation.9 | async-start | bytes 9437184 | tf_op jit(solution)/shard_map/psum | solution.py:161
  9.5 69.2 %copy-start.60 = (f32[128]{0:T(128)}, f32[128]{0:T(128)S(1)}, u32[]{:S(2)}) copy-start(f32[128]{0:T(128)S(1)} %multiply_power_fusion) | copy-start | bytes 1540
  38.4 40.3 %copy-start.45 = (f32[1024]{0:T(1024)}, f32[1024]{0:T(1024)S(1)}, u32[]{:S(2)}) copy-start(f32[1024]{0:T(1024)S(1)} %convert_element_type.215) | copy-start | bytes 12292
  38.4 49.7 %copy-start.56 = (f32[256]{0:T(256)}, f32[256]{0:T(256)S(1)}, u32[]{:S(2)}) copy-start(f32[256]{0:T(256)S(1)} %convert_add_fusion.6) | copy-start | bytes 3076
  83.7 14.7 %collective-permute-start = (bf16[511,512]{0,1:T(8,128)(2,1)}, bf16[511,512]{0,1:T(8,128)(2,1)}, u32[]{:S(2)}, u32[]{:S(2)}) collective-permute-start(bf16[511,512]{0,1:T(8,128)(2,1)} %pad_maximum_fusion.6), channel_id=1, source_target_pairs={{0,2},{2,4},{4,6},{1,3},{3,5},{5,7},{8,10},{10,12},{12,14},{9,11},... | collective-permute-start | bytes 1569800 | tf_op jit(solution)/shard_map/ppermute | solution.py:19
  144.4 116.9 %all-gather.13.cloned.1.call-start = ((), (), s32[]{:S(2)}) async-start(), calls=%async_computation.10 | async-start | bytes 9953280 | tf_op jit(solution)/shard_map/all_gather | solution.py:94
  145.0 201.9 %all-gather.15.cloned.1.call-start = ((), (), s32[]{:S(2)}) async-start(), calls=%async_computation.11 | async-start | bytes 9953280 | tf_op jit(solution)/shard_map/all_gather | solution.py:95
  145.6 287.2 %all-gather.17.cloned.1.call-start = ((), (), s32[]{:S(2)}) async-start(), calls=%async_computation.12 | async-start | bytes 9953280 | tf_op jit(solution)/shard_map/all_gather | solution.py:96
  146.3 323.4 %all-reduce.25.cloned.1.call-start = ((), (), s32[]{:S(2)}) async-start(), calls=%async_computation.13 | async-start | bytes 4718592 | tf_op jit(solution)/shard_map/psum | solution.py:170
  182.0 164.9 %copy-start.22 = (bf16[1024,1152]{1,0:T(8,128)(2,1)}, bf16[1024,1152]{1,0:T(8,128)(2,1)S(1)}, u32[]{:S(2)}) copy-start(bf16[1024,1152]{1,0:T(8,128)(2,1)S(1)} %multiply_convert_fusion.3) | copy-start | bytes 7077892
  447.8 109.8 %all-reduce.27.cloned.1.call-start = ((), (), s32[]{:S(2)}) async-start(), calls=%async_computation.14 | async-start | bytes 4718592 | tf_op jit(solution)/shard_map/psum | solution.py:184
  534.5 152.7 %all-reduce.31.cloned.1.call-start = ((), (), s32[]{:S(2)}) async-start(), calls=%async_computation.22 | async-start | bytes 7864320 | tf_op jit(solution)/shard_map/psum | solution.py:251
  660.9 102.7 %reduce-scatter.11.cloned.1.call-start = ((), (), s32[]{:S(2)}) async-start(), calls=%async_computation.17 | async-start | bytes 1474560 | tf_op jit(solution)/shard_map/reduce_scatter | solution.py:280
  665.8 97.8 %reduce-scatter.7.cloned.1.call-start = ((), (), s32[]{:S(2)}) async-start(), calls=%async_computation.15 | async-start | bytes 1474560 | tf_op jit(solution)/shard_map/reduce_scatter | solution.py:274
  669.8 114.7 %reduce-scatter.9.cloned.1.call-start = ((), (), s32[]{:S(2)}) async-start(), calls=%async_computation.16 | async-start | bytes 1474560 | tf_op jit(solution)/shard_map/reduce_scatter | solution.py:277
  688.5 16.0 %collective-permute-start.1 = (bf16[511,512]{0,1:T(8,128)(2,1)S(1)}, bf16[511,512]{0,1:T(8,128)(2,1)S(1)}, u32[]{:S(2)}, u32[]{:S(2)}) collective-permute-start(bf16[511,512]{0,1:T(8,128)(2,1)S(1)} %slice.113), channel_id=1, source_target_pairs={{2,0},{4,2},{6,4},{3,1},{5,3},{7,5},{10,8},{12,10},{14,12},{11,9},... | collective-permute-start | bytes 1569800 | tf_op jit(solution)/shard_map/ppermute | solution.py:19
  719.0 151.8 %reduce-scatter.17.cloned.1.call-start = ((), (), s32[]{:S(2)}) async-start(), calls=%async_computation.20 | async-start | bytes 9953280 | tf_op jit(solution)/shard_map/reduce_scatter | solution.py:289
  733.8 223.2 %reduce-scatter.13.cloned.1.call-start = ((), (), s32[]{:S(2)}) async-start(), calls=%async_computation.18 | async-start | bytes 9953280 | tf_op jit(solution)/shard_map/reduce_scatter | solution.py:283
  749.4 293.8 %reduce-scatter.15.cloned.1.call-start = ((), (), s32[]{:S(2)}) async-start(), calls=%async_computation.19 | async-start | bytes 9953280 | tf_op jit(solution)/shard_map/reduce_scatter | solution.py:286
  763.3 281.3 %copy-start.12 = (bf16[1024,1152]{1,0:T(8,128)(2,1)S(1)}, bf16[1024,1152]{1,0:T(8,128)(2,1)}, u32[]{:S(2)}) copy-start(bf16[1024,1152]{1,0:T(8,128)(2,1)} %param.21) | copy-start | bytes 7077892
  763.3 524.6 %all-reduce.29.cloned.1.call-start = ((), (), s32[]{:S(2)}) async-start(), calls=%async_computation.21 | async-start | bytes 13713408 | tf_op jit(solution)/shard_map/psum | solution.py:312
  (67 other events, 597.6 us)
Sparse Core Ops, SparseCore 0:
  9.8 30.6 all-gather.6
  42.3 27.5 all-gather.8
  71.8 27.5 all-gather.10
  144.5 29.8 all-reduce.22
  176.1 85.1 all-gather.12
  263.0 83.9 all-gather.14
  348.8 83.9 all-gather.16
  447.9 21.7 all-reduce.24
  534.7 22.9 all-reduce.26
  661.0 26.1 all-reduce.30
  690.2 29.9 reduce-scatter.10
  723.5 28.7 reduce-scatter.6
  755.8 28.7 reduce-scatter.8
  787.5 83.2 reduce-scatter.16
  873.7 83.2 reduce-scatter.12
  959.9 83.2 reduce-scatter.14
  1045.9 241.9 all-reduce.28
where the time goes:
time: 1310 us
  waiting for transfers between devices  824 us (63%)
  matrix products  230 us (18%)
  other arithmetic  84.9 us (6%)
  local copies, waits for them, and re-layouts  78.8 us (6%)
  blocking collectives  48.6 us (4%)
  between operations  17.6 us (1%)
  loops' own time  13.2 us (1%)
    psum x1, waiting for transfers between devices, shards(): lax.psum(query_share.astype(jnp.bfloat16), 'ctx').astype(jnp.float32)  198 us
    reduce_scatter x1, waiting for transfers between devices, shards(): lax.psum_scatter(down_weight_grad.astype(jnp.bfloat16), 'fsdp', scatter_d...  86.2 us
    reduce_scatter x1, waiting for transfers between devices, shards(): lax.psum_scatter(up_weight_grad.astype(jnp.bfloat16), 'fsdp', scatter_dim...  86.2 us
    reduce_scatter x1, waiting for transfers between devices, shards(): lax.psum_scatter(gate_weight_grad.astype(jnp.bfloat16), 'fsdp', scatter_d...  86.2 us
    all_gather x1, waiting for transfers between devices, shards(): lax.all_gather(gate_weight, 'fsdp', axis=0, tiled=True)  79.2 us
    all_gather x1, waiting for transfers between devices, shards(): lax.all_gather(up_weight, 'fsdp', axis=0, tiled=True)  70.9 us
    dot_general x6, matrix products, inner_cols(): lax.dot_general(left, right, (((1,), (1,)), ((), ())), preferred_element_...  69.6 us
    all_gather x1, waiting for transfers between devices, shards(): lax.all_gather(down_weight, 'fsdp', axis=1, tiled=True)  65.2 us
  transfers between devices with their start and end apart: 19, of which 16 were waited for; matrix products, arithmetic and copies ran while one was open for 15% of the time, Pallas kernels for 0%

commit v1 on v0

v1 whole, which is shorter than its diff:
```python
import jax
import jax.numpy as jnp
from jax import lax
from jax.sharding import PartitionSpec as P


WINDOW = 512
EPS = 1e-06
SCALE = 0.0625
NEG = -1e30
F32 = jnp.float32
BF16 = jnp.bfloat16


def tied(value, *others):
    return lax.optimization_barrier((value,) + others)[0]


def passed_along(value, axis, steps):
    count = lax.axis_size(axis)
    first, last = (max(0, -steps), min(count, count - steps))
    return lax.ppermute(value, axis, [(source, source + steps) for source in range(first, last)])


def hop(value, axis, flip):
    return lax.ppermute(value, axis, [(i, i ^ flip) for i in range(lax.axis_size(axis))])


def summed_tp(part):
    if lax.axis_size("tp") != 2:
        return lax.psum(part, "tp").astype(F32)
    return part.astype(F32) + hop(part, "tp", 1).astype(F32)


def put_rows(full, rows, start):
    return lax.dynamic_update_slice_in_dim(full, rows, start, 0)


def on_square():
    return lax.axis_size("fsdp") == 4


def gather_start(shard):
    if not on_square():
        return (shard,)
    return (shard, hop(shard, "fsdp", 1), hop(shard, "fsdp", 2))


def gather_finish(first):
    shard, near, side = first
    half = shard.shape[0] // 2
    far_top = hop(side[:half], "fsdp", 1)
    far_low = hop(near[half:], "fsdp", 2)
    return (shard, near, side, far_top, far_low)


def placed(pieces, keep):
    shard, near, side, far_top, far_low = pieces
    half = far_top.shape[0]
    me = lax.axis_index("fsdp")
    full = jnp.zeros((4 * keep,) + shard.shape[1:], shard.dtype)
    full = put_rows(full, shard[:keep], me * keep)
    full = put_rows(full, near[:keep], (me ^ 1) * keep)
    full = put_rows(full, side[:keep], (me ^ 2) * keep)
    full = put_rows(full, far_top, (me ^ 3) * keep)
    return put_rows(full, far_low[: keep - half], (me ^ 3) * keep + half)


def assisted():
    return on_square() and lax.axis_size("ctx") % 2 == 0


def wide_start(shard):
    if not assisted():
        return gather_start(shard)
    third = shard.shape[0] // 3
    odd = lax.axis_index("ctx") % 2
    mine = lax.dynamic_slice_in_dim(shard, odd * third, third, 0)
    part = jnp.concatenate([mine, shard[2 * third :]], axis=0)
    return (shard, hop(part, "fsdp", 1), hop(part, "fsdp", 2))


def wide_finish(first):
    if not on_square():
        return lax.all_gather(first[0], "fsdp", axis=0, tiled=True)
    if not assisted():
        return placed(gather_finish(first), first[0].shape[0])
    shard, near, side = first
    rows = shard.shape[0]
    third = rows // 3
    odd = lax.axis_index("ctx") % 2
    me = lax.axis_index("fsdp")
    far_mine = hop(side[:third], "fsdp", 1)
    far_rest = hop(near[third:], "fsdp", 2)
    others = hop(jnp.concatenate([near[:third], side[:third]], axis=0), "ctx", 1)
    far_other = hop(far_mine, "ctx", 1)
    full = jnp.zeros((4 * rows,) + shard.shape[1:], shard.dtype)
    full = put_rows(full, shard, me * rows)
    for flip, mine, other, rest in (
        (1, near[:third], others[:third], near[third:]),
        (2, side[:third], others[third:], side[third:]),
        (3, far_mine, far_other, far_rest),
    ):
        base = (me ^ flip) * rows
        full = put_rows(full, mine, base + odd * third)
        full = put_rows(full, other, base + (1 - odd) * third)
        full = put_rows(full, rest, base + 2 * third)
    return full


def scatter_rows(full, hops):
    if not (hops and on_square()):
        return lax.psum_scatter(full, "fsdp", scatter_dimension=0, tiled=True)
    rows = full.shape[0] // 4
    half = rows // 2
    me = lax.axis_index("fsdp")

    def part(flip, start, size):
        return lax.dynamic_slice_in_dim(full, (me ^ flip) * rows + start, size, 0)

    for_side = hop(part(3, 0, half), "fsdp", 1)
    for_near = hop(part(3, half, rows - half), "fsdp", 2)
    to_near = jnp.concatenate([part(1, 0, half), part(1, half, rows - half) + for_near], axis=0)
    to_side = jnp.concatenate([part(2, 0, half) + for_side, part(2, half, rows - half)], axis=0)
    from_near = hop(to_near, "fsdp", 1)
    from_side = hop(to_side, "fsdp", 2)
    return (
        part(0, 0, rows).astype(F32) + from_near.astype(F32) + from_side.astype(F32)
    ).astype(BF16)


def summed_gains(parts):
    if not (on_square() and lax.axis_size("ctx") == 4):
        whole = lax.psum(parts, ("fsdp", "ctx"))
        return lax.dynamic_index_in_dim(whole, lax.axis_index("fsdp"), 0, keepdims=False)
    me = lax.axis_index("fsdp")

    def part(flip):
        return lax.dynamic_slice_in_dim(parts, me ^ flip, 1, 0)

    mine = part(0)
    for flip in (1, 2, 3):
        mine = mine + hop(part(flip), "fsdp", flip)
    one, two, three = (hop(mine, "ctx", flip) for flip in (1, 2, 3))
    return ((mine + one) + (two + three))[0]


def summed_ctx(share, chunks):
    if chunks == 0 or lax.axis_size("ctx") != 4:
        return lax.psum(share, "ctx")
    here = lax.axis_index("ctx")
    rows = share.shape[0] // chunks
    pieces = []
    for i in range(chunks):
        part = share[i * rows : (i + 1) * rows]
        inward = lax.ppermute(part, "ctx", [(0, 1), (3, 2)])
        pair = part + inward
        across = lax.ppermute(pair, "ctx", [(1, 2), (2, 1)])
        total = pair + across
        outward = lax.ppermute(total, "ctx", [(1, 0), (2, 3)])
        pieces.append(jnp.where((here == 0) | (here == 3), outward, total))
    return jnp.concatenate(pieces, axis=0)


def reduced(full, hops, chunks):
    return summed_ctx(scatter_rows(full, hops), chunks).astype(F32)


def normalize(values):
    inverse = lax.rsqrt(jnp.mean(values * values, axis=-1, keepdims=True) + EPS)
    return (values * inverse, inverse)


def norm_back(gradient, normed, inverse):
    return inverse * (gradient - normed * jnp.mean(gradient * normed, axis=-1, keepdims=True))


def rotate(values, cosine_table, sine_table):
    half_width = values.shape[-1] // 2
    front_half = values[..., :half_width]
    back_half = values[..., half_width:]
    return jnp.concatenate(
        [
            front_half * cosine_table - back_half * sine_table,
            back_half * cosine_table + front_half * sine_table,
        ],
        axis=-1,
    )


def rotary(positions, head_width):
    half_width = head_width // 2
    frequency = 10000.0 ** (-(2.0 * jnp.arange(half_width).astype(F32)) / head_width)
    angles = positions.astype(F32)[:, None] * frequency[None, :]
    return (jnp.cos(angles), jnp.sin(angles))


def product(left, right):
    return jnp.dot(left, right, preferred_element_type=F32)


def inner_rows(left, right):
    return lax.dot_general(left, right, (((0,), (0,)), ((), ())), preferred_element_type=F32)


def inner_cols(left, right):
    return lax.dot_general(left, right, (((1,), (1,)), ((), ())), preferred_element_type=F32)


def layer(
    tokens,
    positions,
    query_weight,
    keyvalue_weight,
    output_weight,
    gate_weight,
    up_weight,
    down_weight,
    input_gain,
    query_gain,
    key_gain,
    attention_gain,
    middle_gain,
    final_gain,
    cotangent,
):
    fsdp = lax.axis_size("fsdp")
    head_width = query_gain.shape[0] * fsdp
    query_width = query_weight.shape[1]
    local_heads = query_width // head_width
    tok_rows = tokens.shape[0]
    block_rows = WINDOW
    block_count = tok_rows // block_rows

    shard_rows = query_weight.shape[0]
    gains = jnp.concatenate(
        [input_gain, attention_gain, middle_gain, final_gain, query_gain, key_gain]
    )
    qkv_shard = jnp.concatenate([query_weight, keyvalue_weight], axis=1)
    output_shard = output_weight.T
    down_shard = down_weight.T
    qkv_first = gather_start(qkv_shard)
    gains = tied(gains[None], qkv_shard)
    if on_square():
        near, side, far = (hop(gains, "fsdp", flip) for flip in (1, 2, 3))
        me = lax.axis_index("fsdp")
        gains_full = jnp.zeros((fsdp, gains.shape[1]), BF16)
        for flip, piece in enumerate((gains, near, side, far)):
            gains_full = put_rows(gains_full, piece, me ^ flip)
        qkv_pieces = gather_finish(qkv_first)
        output_first = gather_start(tied(output_shard, *qkv_pieces[3:]))
        gate_first = wide_start(tied(gate_weight, *qkv_pieces[3:]))
        up_first = wide_start(tied(up_weight, *gate_first[1:]))
        down_first = wide_start(tied(down_shard, *up_first[1:]))
        qkv_full = placed(qkv_pieces, shard_rows)
        output_full = placed(gather_finish(output_first), shard_rows)
    else:
        gains_full = lax.all_gather(gains, "fsdp", axis=0, tiled=True)
        qkv_full = lax.all_gather(qkv_shard, "fsdp", axis=0, tiled=True)
        output_full = lax.all_gather(output_shard, "fsdp", axis=0, tiled=True)
        gate_first, up_first, down_first = (gate_weight,), (up_weight,), (down_shard,)
    gate_full = wide_finish(gate_first)
    up_full = wide_finish(up_first)
    down_full = wide_finish(down_first)
    cuts = [0, shard_rows, 2 * shard_rows, 3 * shard_rows, 4 * shard_rows]
    cuts += [cuts[-1] + query_gain.shape[0], cuts[-1] + query_gain.shape[0] + key_gain.shape[0]]
    factors = [
        1.0 + gains_full[:, low:high].reshape(-1).astype(F32)
        for low, high in zip(cuts[:-1], cuts[1:])
    ]
    input_factor, attention_factor, middle_factor, final_factor, query_factor, key_factor = factors

    inputs = tokens.astype(F32)
    normed_in, inverse_in = normalize(inputs)
    hidden = (normed_in * input_factor).astype(BF16)
    qkv_raw = product(hidden, qkv_full)
    query_raw = qkv_raw[:, :query_width].reshape(tok_rows, local_heads, head_width)
    keyvalue_raw = qkv_raw[:, query_width:]
    cosine_table, sine_table = rotary(positions, head_width)
    cosine_heads = cosine_table[:, None, :]
    sine_heads = sine_table[:, None, :]
    query_normed, query_inverse = normalize(query_raw)
    query_rot = rotate(query_normed * query_factor, cosine_heads, sine_heads).astype(BF16)
    key_normed, key_inverse = normalize(keyvalue_raw[:, :head_width])
    key_rot = rotate(key_normed * key_factor, cosine_table, sine_table)
    keyvalue = jnp.concatenate([key_rot, keyvalue_raw[:, head_width:]], axis=1).astype(BF16)
    earlier = passed_along(keyvalue[tok_rows - WINDOW :], "ctx", 1)

    lag = (
        lax.broadcasted_iota(jnp.int32, (block_rows, 2 * WINDOW), 0)
        - lax.broadcasted_iota(jnp.int32, (block_rows, 2 * WINDOW), 1)
        + WINDOW
    )
    reach = jnp.minimum(positions, WINDOW - 1)[:, None]

    def block_of(index):
        rows = slice(index * block_rows, (index + 1) * block_rows)
        if index == 0:
            slab = jnp.concatenate([earlier, keyvalue[:block_rows]], axis=0)
        else:
            slab = keyvalue[(index - 1) * block_rows : (index + 1) * block_rows]
        query_block = query_rot[rows]
        key_block = slab[:, :head_width]
        value_block = slab[:, head_width:]
        allowed = (lag >= 0) & (lag <= reach[rows])
        scores = (
            jnp.einsum("rhd,sd->hrs", query_block, key_block, preferred_element_type=F32) * SCALE
        )
        return query_block, key_block, value_block, jnp.where(allowed[None], scores, NEG)

    mixed = [None] * block_count
    logsums = [None] * block_count
    for index in reversed(range(block_count)):
        _, _, value_block, scores = block_of(index)
        highest = jnp.max(scores, axis=-1, keepdims=True)
        shifted = jnp.exp(scores - highest)
        totals = jnp.sum(shifted, axis=-1, keepdims=True)
        weights = (shifted / totals).astype(BF16)
        mixed[index] = jnp.einsum(
            "hrs,sd->rhd", weights, value_block, preferred_element_type=F32
        ).astype(BF16)
        logsums[index] = highest + jnp.log(totals)
    attended = jnp.concatenate(mixed, axis=0).reshape(tok_rows, query_width)
    branch = inner_cols(attended, output_full).astype(BF16)
    branch = summed_tp(branch)
    branch_normed, branch_inverse = normalize(branch)
    residual = inputs + branch_normed * attention_factor
    middle_normed, middle_inverse = normalize(residual)
    hidden_ffn = (middle_normed * middle_factor).astype(BF16)

    gate_value = product(hidden_ffn, gate_full)
    up_value = product(hidden_ffn, up_full)
    activated, gelu_pull = jax.vjp(lambda v: jax.nn.gelu(v, approximate=True), gate_value)
    feed = (activated * up_value).astype(BF16)
    outcome = inner_cols(feed, down_full).astype(BF16)
    outcome = summed_tp(outcome)
    outcome_normed, outcome_inverse = normalize(outcome)
    layer_out = (residual + outcome_normed * final_factor).astype(BF16)
    upstream = cotangent.astype(F32)
    final_gain_grad = jnp.sum(upstream * outcome_normed, axis=0)
    outcome_grad = norm_back(upstream * final_factor, outcome_normed, outcome_inverse).astype(BF16)
    down_grad = inner_rows(outcome_grad, feed).astype(BF16)
    outcome_grad = tied(outcome_grad, down_grad)
    feed_grad = product(outcome_grad, down_full)
    gate_grad = gelu_pull(feed_grad * up_value)[0].astype(BF16)
    up_grad = (feed_grad * activated).astype(BF16)
    gate_weight_grad = inner_rows(hidden_ffn, gate_grad).astype(BF16)
    up_grad = tied(up_grad, gate_weight_grad)
    up_weight_grad = inner_rows(hidden_ffn, up_grad).astype(BF16)
    gate_grad, up_grad, _ = lax.optimization_barrier((gate_grad, up_grad, up_weight_grad))
    hidden_part = inner_cols(gate_grad, gate_full)
    hidden_part = (hidden_part + inner_cols(up_grad, up_full)).astype(BF16)
    hidden_ffn_grad = summed_tp(hidden_part)
    middle_gain_grad = jnp.sum(hidden_ffn_grad * middle_normed, axis=0)
    residual_grad = upstream + norm_back(
        hidden_ffn_grad * middle_factor, middle_normed, middle_inverse
    )
    attention_gain_grad = jnp.sum(residual_grad * branch_normed, axis=0)
    branch_grad = norm_back(
        residual_grad * attention_factor, branch_normed, branch_inverse
    ).astype(BF16)
    output_weight_grad = inner_rows(branch_grad, attended).astype(BF16)

    attended_grad = product(branch_grad, output_full).astype(BF16)
    attended_heads = attended_grad.reshape(tok_rows, local_heads, head_width)
    query_parts = [None] * block_count
    slab_grads = [None] * block_count
    for index in range(block_count):
        query_block, key_block, value_block, scores = block_of(index)
        weights = jnp.exp(scores - logsums[index])
        upper_grad = attended_heads[index * block_rows : (index + 1) * block_rows]
        weight_grad = jnp.einsum(
            "rhd,sd->hrs", upper_grad, value_block, preferred_element_type=F32
        )
        centred = jnp.sum(weights * weight_grad, axis=-1, keepdims=True)
        score_grad = (weights * (weight_grad - centred)).astype(BF16)
        query_parts[index] = (
            jnp.einsum("hrs,sd->rhd", score_grad, key_block, preferred_element_type=F32) * SCALE
        )
        key_part = (
            jnp.einsum("hrs,rhd->sd", score_grad, query_block, preferred_element_type=F32) * SCALE
        )
        value_part = jnp.einsum(
            "hrs,rhd->sd", weights.astype(BF16), upper_grad, preferred_element_type=F32
        )
        slab_grads[index] = jnp.concatenate([key_part, value_part], axis=1)
    returned = passed_along(slab_grads[0][:WINDOW].astype(BF16), "ctx", -1)
    own_grads = []
    for index in range(block_count):
        rows = slab_grads[index][WINDOW:]
        if index + 1 < block_count:
            rows = rows + slab_grads[index + 1][:WINDOW]
        else:
            rows = rows + returned.astype(F32)
        own_grads.append(rows)
    keyvalue_grad = summed_tp(jnp.concatenate(own_grads, axis=0).astype(BF16))

    query_turned = jnp.concatenate(query_parts, axis=0)
    query_unturned = rotate(query_turned, cosine_heads, -sine_heads)
    query_gain_part = jnp.sum(query_unturned * query_normed, axis=(0, 1))
    query_raw_grad = (
        norm_back(query_unturned * query_factor, query_normed, query_inverse)
        .reshape(tok_rows, query_width)
        .astype(BF16)
    )
    key_unturned = rotate(keyvalue_grad[:, :head_width], cosine_table, -sine_table)
    key_gain_grad = jnp.sum(key_unturned * key_normed, axis=0)
    key_raw_grad = norm_back(key_unturned * key_factor, key_normed, key_inverse)
    keyvalue_raw_grad = jnp.concatenate(
        [key_raw_grad, keyvalue_grad[:, head_width:]], axis=1
    ).astype(BF16)
    query_part = inner_cols(query_raw_grad, qkv_full[:, :query_width]).astype(BF16)
    qkv_weight_grad = inner_rows(
        hidden, jnp.concatenate([query_raw_grad, keyvalue_raw_grad], axis=1)
    ).astype(BF16)
    hidden_kv = inner_cols(keyvalue_raw_grad, qkv_full[:, query_width:])
    hidden_grad = summed_tp(query_part) + hidden_kv
    input_gain_grad = jnp.sum(hidden_grad * normed_in, axis=0)
    tokens_grad = (
        residual_grad + norm_back(hidden_grad * input_factor, normed_in, inverse_in)
    ).astype(BF16)

    down_share = reduced(down_grad, True, 1).T
    gate_share = reduced(gate_weight_grad, True, 1)
    up_share = reduced(up_weight_grad, False, 3)
    attention_shares = reduced(
        jnp.concatenate([qkv_weight_grad, output_weight_grad], axis=1), True, 1
    )
    query_gain_grad = summed_tp(query_gain_part)
    gain_shares = summed_gains(
        jnp.concatenate(
            [
                grad.reshape(fsdp, -1)
                for grad in (
                    input_gain_grad,
                    attention_gain_grad,
                    middle_gain_grad,
                    final_gain_grad,
                    query_gain_grad,
                    key_gain_grad,
                )
            ],
            axis=1,
        )
    )
    gain_shares = [gain_shares[low:high] for low, high in zip(cuts[:-1], cuts[1:])]
    input_share, attention_share, middle_share, final_share, query_gshare, key_share = gain_shares
    qkv_width = qkv_shard.shape[1]
    qkv_share = attention_shares[:, :qkv_width]
    output_share = attention_shares[:, qkv_width:].T
    return (
        layer_out,
        tokens_grad,
        qkv_share[:, :query_width],
        qkv_share[:, query_width:],
        output_share,
        gate_share,
        up_share,
        down_share,
        input_share,
        query_gshare,
        key_share,
        attention_share,
        middle_share,
        final_share,
    )


def solution(mesh):
    rows = P(("fsdp", "ctx"), None)
    inward = P("fsdp", "tp")
    outward = P("tp", "fsdp")
    gain = P("fsdp")
    whole = P("fsdp", None)
    return jax.shard_map(
        layer,
        mesh=mesh,
        in_specs=(
            (rows, P(("fsdp", "ctx")), inward, whole, outward, inward, inward, outward)
            + (gain,) * 6
            + (rows,)
        ),
        out_specs=(rows, rows, inward, whole, outward, inward, inward, outward) + (gain,) * 6,
        check_vma=False,
    )
```

time: 1310 us -> 959 us (0.73)
  waiting for transfers between devices: 824 us -> 360 us
  starting transfers between devices: 7.93 us -> 177 us
  matrix products: 230 us -> 170 us
  blocking collectives: 48.6 us -> 0 us
  other arithmetic: 84.9 us -> 116 us
  local copies, waits for them, and re-layouts: 78.8 us -> 109 us
  loops' own time: 13.2 us -> 0 us
    ppermute x0 -> x71, waiting for transfers between devices: none -> 355 us  [the longest x53 186 us: hop(): lax.ppermute(value, axis, [(i, i ^ flip) for i in range(lax.axis_size(axi...]
    psum x5 -> x0, waiting for transfers between devices: 286 us -> none  [the longest x1 198 us: shards(): lax.psum(query_share.astype(jnp.bfloat16), 'ctx').astype(jnp.float32)]
    reduce_scatter x6 -> x1, waiting for transfers between devices: 280 us -> 0.02 us  [scatter_rows(): return lax.psum_scatter(full, 'fsdp', scatter_dimension=0, tiled=True)]
    all_gather x6 -> x0, waiting for transfers between devices: 242 us -> none  [the longest x1 79.2 us: shards(): lax.all_gather(gate_weight, 'fsdp', axis=0, tiled=True)]
    ppermute x0 -> x71, starting transfers between devices: none -> 171 us  [the longest x53 137 us: hop(): lax.ppermute(value, axis, [(i, i ^ flip) for i in range(lax.axis_size(axi...]
    unnamed x2 -> x0, blocking collectives: 33.5 us -> none
    dot_general x20 -> x17, matrix products: 108 us -> 76.6 us  [the longest x5 59.6 us: product(): return jnp.dot(left, right, preferred_element_type=F32)]
    dot_general x6, matrix products: 69.6 us -> 54.1 us  [inner_cols(): lax.dot_general(left, right, (((1,), (1,)), ((), ())), preferred_element_...]
  transfers between devices with their start and end apart: 19 -> 74, of which waited for: 16 -> 30; matrix products, arithmetic and copies ran while one was open for 15% -> 29% of each run, Pallas kernels for 0% -> 0%
where the time goes in v1:
time: 959 us; the launch traced here: 949 us
  waiting for transfers between devices  360 us (38%)
  starting transfers between devices  177 us (18%)
  matrix products  170 us (18%)
  other arithmetic  116 us (12%)
  local copies, waits for them, and re-layouts  109 us (11%)
  between operations  16.5 us (2%)
    ppermute x53, waiting for transfers between devices, hop(): lax.ppermute(value, axis, [(i, i ^ flip) for i in range(lax.axis_size(axi...  186 us
    ppermute x53, starting transfers between devices, hop(): lax.ppermute(value, axis, [(i, i ^ flip) for i in range(lax.axis_size(axi...  137 us
    ppermute x6, waiting for transfers between devices, summed_ctx(): outward = lax.ppermute(total, 'ctx', [(1, 0), (2, 3)])  136 us
    dot_general x5, matrix products, product(): return jnp.dot(left, right, preferred_element_type=F32)  59.6 us
    dot_general x6, matrix products, inner_cols(): lax.dot_general(left, right, (((1,), (1,)), ((), ())), preferred_element_...  54.1 us
    dot_general x5, matrix products, inner_rows(): lax.dot_general(left, right, (((0,), (0,)), ((), ())), preferred_element_...  39.8 us
    dynamic_update_slice x41, local copies, waits for them, and re-layouts, put_rows(): return lax.dynamic_update_slice_in_dim(full, rows, start, 0)  34.2 us
    ppermute x6, waiting for transfers between devices, summed_ctx(): inward = lax.ppermute(part, 'ctx', [(0, 1), (3, 2)])  33.3 us
  transfers between devices with their start and end apart: 74, of which 30 were waited for; matrix products, arithmetic and copies ran while one was open for 29% of the time, Pallas kernels for 0%

profile of v1, /device:TPU:0, one launch (start us, length us, event | category | flops | bytes accessed | tf_op | source)
XLA Modules:
  0.0 949.5 jit_solution(9068378655085266657)
XLA Ops:
  113.5 33.7 %collective-permute-done.16 = bf16[96,3456]{1,0:T(8,128)(2,1)S(1)} collective-permute-done((bf16[96,3456]{1,0:T(8,128)(2,1)S(1)}, bf16[96,3456]{1,0:T(8,128)(2,1)S(1)}, u32[]{:S(2)}, u32[]{:S(2)}) %collective-permute-start.16) | collective-permute-done | bytes 663584 | tf_op jit(solution)/shard_map/ppermute | solution.py:26
  153.5 25.6 %collective-permute-done.15 = bf16[192,3456]{1,0:T(8,128)(2,1)S(1)} collective-permute-done((bf16[192,3456]{1,0:T(8,128)(2,1)S(1)}, bf16[192,3456]{1,0:T(8,128)(2,1)S(1)}, u32[]{:S(2)}, u32[]{:S(2)}) %collective-permute-start.15) | collective-permute-done | bytes 1327136 | tf_op jit(solution)/shard_map/ppermute | solution.py:26
  185.0 6.8 collective-permute-done.17
  205.6 12.3 %fusion.153 = f32[1024,3456]{1,0:T(8,128)} fusion(bf16[1024,1152]{1,0:T(8,128)(2,1)S(1)} %multiply_convert_fusion.3, bf16[1152,3456]{1,0:T(8,128)(2,1)S(1)} %constant_dynamic-update-slice_fusion.14), kind=kOutput, calls=%fused_computation.363 | convolution fusion | flops 8153726976 | bytes 24477696 | tf_op jit(solution)/shard_map/dot_general | solution.py:199
  247.3 19.7 %multiply_convert_fusion.1 = (bf16[1024,3456]{1,0:T(8,128)(2,1)}, f32[1024,3456]{1,0:T(8,128)}) fusion(f32[1024,3456]{1,0:T(8,128)} %fusion.153, bf16[1024,1152]{1,0:T(8,128)(2,1)} %copy-done.44, bf16[1152,3456]{1,0:T(8,128)(2,1)} %constant_dynamic-update-slice_fusion.7), kind=kOutput, calls=%fused_computation.13 | convolution fusion | flops 8189116416 | bytes 45711360 | tf_op jit(solution)/shard_map/dot_general | solution.py:199
  289.7 11.0 %convolution_convert_fusion.3 = bf16[1024,1152]{1,0:T(8,128)(2,1)} fusion(bf16[1024,3456]{1,0:T(8,128)(2,1)S(1)} %copy-done.100, bf16[1152,3456]{1,0:T(8,128)(2,1)S(1)} %constant_dynamic-update-slice_fusion), kind=kOutput, calls=%fused_computation.92 | convolution fusion | flops 8154906624 | bytes 17399808 | tf_op jit(solution)/shard_map/dot_general | solution.py:207
  319.5 12.4 %convolution_convert_fusion.2 = bf16[1152,3456]{1,0:T(8,128)(2,1)S(1)} fusion(bf16[1024,1152]{1,0:T(8,128)(2,1)S(1)} %get-tuple-element.28, bf16[1024,3456]{1,0:T(8,128)(2,1)} %get-tuple-element.179), kind=kOutput, calls=%fused_computation.4 | convolution fusion | flops 8157708288 | bytes 17399808 | tf_op jit(solution)/shard_map/dot_general | solution.py:203
  336.3 21.3 %multiply_convert_fusion = (bf16[1024,3456]{1,0:T(8,128)(2,1)}, bf16[1024,3456]{1,0:T(8,128)(2,1)}) fusion(f32[1024,3456]{1,0:T(8,128)} %fusion.153, f32[1024,3456]{1,0:T(8,128)} %get-tuple-element.180, bf16[1024,1152]{1,0:T(8,128)(2,1)S(1)} %get-tuple-element.28, bf16[1152,3456]{1,0:T(8,128)(2,1)S(1)} %bitcast.151), kind=kOutput, calls=%fused_computation.12 | convolution fusion | flops 8238661632 | bytes 52789248 | tf_op jit(solution)/shard_map/dot_general | solution.py:199
  357.6 11.9 %convolution_convert_fusion.1 = bf16[1152,3456]{1,0:T(8,128)(2,1)S(1)} fusion(bf16[1024,1152]{1,0:T(8,128)(2,1)} %copy-done.44, bf16[1024,3456]{1,0:T(8,128)(2,1)} %get-tuple-element.30), kind=kOutput, calls=%fused_computation.3 | convolution fusion | flops 8157708288 | bytes 17399808 | tf_op jit(solution)/shard_map/dot_general | solution.py:203
  374.0 11.1 %convolution_convert_fusion = bf16[1152,3456]{1,0:T(8,128)(2,1)} fusion(bf16[1024,1152]{1,0:T(8,128)(2,1)S(1)} %copy-done.45, bf16[1024,3456]{1,0:T(8,128)(2,1)S(1)} %copy-done.101), kind=kOutput, calls=%fused_computation.2 | convolution fusion | flops 8157708288 | bytes 17399808 | tf_op jit(solution)/shard_map/dot_general | solution.py:203
  389.2 17.2 %fusion.154 = f32[1024,1152]{1,0:T(8,128)} fusion(bf16[1024,3456]{1,0:T(8,128)(2,1)} %get-tuple-element.31, bf16[1152,3456]{1,0:T(8,128)(2,1)} %constant_dynamic-update-slice_fusion.7), kind=kOutput, calls=%fused_computation.364 | convolution fusion | flops 8153726976 | bytes 19759104 | tf_op jit(solution)/shard_map/dot_general | solution.py:207
  406.4 12.9 %add_convert_fusion = bf16[1024,1152]{1,0:T(8,128)(2,1)S(1)} fusion(f32[1024,1152]{1,0:T(8,128)} %fusion.154, bf16[1024,3456]{1,0:T(8,128)(2,1)} %get-tuple-element.30, bf16[1152,3456]{1,0:T(8,128)(2,1)S(1)} %bitcast.153), kind=kOutput, calls=%fused_computation.53 | convolution fusion | flops 8156086272 | bytes 22118400 | tf_op jit(solution)/shard_map/dot_general | solution.py:207
  419.4 8.7 collective-permute-done.61
  438.0 32.8 %collective-permute-done.45 = bf16[144,3456]{1,0:T(8,128)(2,1)} collective-permute-done((bf16[144,3456]{1,0:T(8,128)(2,1)}, bf16[144,3456]{1,0:T(8,128)(2,1)}, u32[]{:S(2)}, u32[]{:S(2)}) %collective-permute-start.45) | collective-permute-done | bytes 995360 | tf_op jit(solution)/shard_map/ppermute | solution.py:26
  556.2 34.6 %collective-permute-done.36 = bf16[144,1536]{1,0:T(8,128)(2,1)} collective-permute-done((bf16[144,1536]{1,0:T(8,128)(2,1)}, bf16[144,1536]{1,0:T(8,128)(2,1)}, u32[]{:S(2)}, u32[]{:S(2)}) %collective-permute-start.36) | collective-permute-done | bytes 442400 | tf_op jit(solution)/shard_map/ppermute | solution.py:26
  636.3 12.1 %collective-permute-done.47 = bf16[288,3456]{1,0:T(8,128)(2,1)} collective-permute-done((bf16[288,3456]{1,0:T(8,128)(2,1)}, bf16[288,3456]{1,0:T(8,128)(2,1)}, u32[]{:S(2)}, u32[]{:S(2)}) %collective-permute-start.47) | collective-permute-done | bytes 1990688 | tf_op jit(solution)/shard_map/ppermute | solution.py:156
  651.8 14.1 %collective-permute-done.40 = bf16[288,1536]{1,0:T(8,128)(2,1)S(1)} collective-permute-done((bf16[288,1536]{1,0:T(8,128)(2,1)}, bf16[288,1536]{1,0:T(8,128)(2,1)S(1)}, u32[]{:S(2)}, u32[]{:S(2)}) %collective-permute-start.40) | collective-permute-done | bytes 884768 | tf_op jit(solution)/shard_map/ppermute | solution.py:156
  677.1 80.1 %collective-permute-start.70 = (f32[1,1280]{1,0:T(1,128)S(1)}, f32[1,1280]{1,0:T(1,128)S(1)}, u32[]{:S(2)}, u32[]{:S(2)}) collective-permute-start(f32[1,1280]{1,0:T(1,128)S(1)} %fusion.129), channel_id=1, source_target_pairs={{0,2},{2,0},{4,6},{6,4},{1,3},{3,1},{5,7},{7,5},{8,10},{10,8},{12,... | collective-permute-start | bytes 15368 | tf_op jit(solution)/shard_map/ppermute | solution.py:26
  769.1 8.2 collective-permute-start.50
  778.6 89.2 %collective-permute-done.42 = bf16[288,1536]{1,0:T(8,128)(2,1)} collective-permute-done((bf16[288,1536]{1,0:T(8,128)(2,1)S(1)}, bf16[288,1536]{1,0:T(8,128)(2,1)}, u32[]{:S(2)}, u32[]{:S(2)}) %collective-permute-start.42) | collective-permute-done | bytes 884768 | tf_op jit(solution)/shard_map/ppermute | solution.py:160
  871.8 7.1 collective-permute-done.53
  893.3 24.5 %collective-permute-done.52 = bf16[96,3456]{1,0:T(8,128)(2,1)S(1)} collective-permute-done((bf16[96,3456]{1,0:T(8,128)(2,1)S(1)}, bf16[96,3456]{1,0:T(8,128)(2,1)S(1)}, u32[]{:S(2)}, u32[]{:S(2)}) %collective-permute-start.52) | collective-permute-done | bytes 663584 | tf_op jit(solution)/shard_map/ppermute | solution.py:160
  917.9 14.2 %collective-permute-done.55 = bf16[96,3456]{1,0:T(8,128)(2,1)S(1)} collective-permute-done((bf16[96,3456]{1,0:T(8,128)(2,1)S(1)}, bf16[96,3456]{1,0:T(8,128)(2,1)S(1)}, u32[]{:S(2)}, u32[]{:S(2)}) %collective-permute-start.55) | collective-permute-done | bytes 663584 | tf_op jit(solution)/shard_map/ppermute | solution.py:160
  932.2 7.7 collective-permute-done.58
  (569 shorter events, 403.7 us)
Async XLA Ops:
  7.2 760.2 %reduce-scatter.2.cloned.1.call-start = ((), (), s32[]{:S(2)}) async-start(), calls=%async_computation.1 | async-start | bytes 9953280 | tf_op jit(solution)/shard_map/reduce_scatter | solution.py:113
  101.0 98.0 %collective-permute-start.12 = (bf16[1024,1152]{1,0:T(8,128)(2,1)S(1)}, bf16[1024,1152]{1,0:T(8,128)(2,1)S(1)}, u32[]{:S(2)}, u32[]{:S(2)}) collective-permute-start(bf16[1024,1152]{1,0:T(8,128)(2,1)S(1)} %convolution_convert_fusion.5), channel_id=1, source_target_pairs={{0,1},{1,0},{2,3},{3,2},{4,5},{5,4},{6,7},{7,6},{8,9},{9,8},{10,11... | collective-permute-start | bytes 7077896 | tf_op jit(solution)/shard_map/ppermute | solution.py:26
  106.4 86.5 %collective-permute-start.18 = (bf16[96,3456]{1,0:T(8,128)(2,1)S(1)}, bf16[96,3456]{1,0:T(8,128)(2,1)S(1)}, u32[]{:S(2)}, u32[]{:S(2)}) collective-permute-start(bf16[96,3456]{1,0:T(8,128)(2,1)S(1)} %get-tuple-element.143), channel_id=1, source_target_pairs={{0,16},{8,24},{16,0},{24,8},{1,17},{9,25},{17,1},{25,9},{2,18},{10... | collective-permute-start | bytes 1990664 | tf_op jit(solution)/shard_map/ppermute | solution.py:26
  150.6 72.1 %collective-permute-start.26 = (bf16[192,3456]{1,0:T(8,128)(2,1)}, bf16[192,3456]{1,0:T(8,128)(2,1)}, u32[]{:S(2)}, u32[]{:S(2)}) collective-permute-start(bf16[192,3456]{1,0:T(8,128)(2,1)} %pad_maximum_fusion.9), channel_id=1, source_target_pairs={{0,16},{8,24},{16,0},{24,8},{1,17},{9,25},{17,1},{25,9},{2,18},{10... | collective-permute-start | bytes 3981320 | tf_op jit(solution)/shard_map/ppermute | solution.py:26
  227.8 57.5 %collective-permute-start.30 = (bf16[96,3456]{1,0:T(8,128)(2,1)}, bf16[96,3456]{1,0:T(8,128)(2,1)}, u32[]{:S(2)}, u32[]{:S(2)}) collective-permute-start(bf16[96,3456]{1,0:T(8,128)(2,1)} %get-tuple-element.140), channel_id=1, source_target_pairs={{0,16},{8,24},{16,0},{24,8},{1,17},{9,25},{17,1},{25,9},{2,18},{10... | collective-permute-start | bytes 1990664 | tf_op jit(solution)/shard_map/ppermute | solution.py:26
  387.5 83.3 %collective-permute-start.45 = (bf16[144,3456]{1,0:T(8,128)(2,1)}, bf16[144,3456]{1,0:T(8,128)(2,1)}, u32[]{:S(2)}, u32[]{:S(2)}) collective-permute-start(bf16[144,3456]{1,0:T(8,128)(2,1)} %get-tuple-element.101), channel_id=1, source_target_pairs={{0,8},{8,0},{16,24},{24,16},{1,9},{9,1},{17,25},{25,17},{2,10},{10... | collective-permute-start | bytes 2985992 | tf_op jit(solution)/shard_map/ppermute | solution.py:26
  388.2 85.4 %collective-permute-start.43 = (bf16[144,3456]{1,0:T(8,128)(2,1)}, bf16[144,3456]{1,0:T(8,128)(2,1)}, u32[]{:S(2)}, u32[]{:S(2)}) collective-permute-start(bf16[144,3456]{1,0:T(8,128)(2,1)} %get-tuple-element.102), channel_id=1, source_target_pairs={{0,16},{8,24},{16,0},{24,8},{1,17},{9,25},{17,1},{25,9},{2,18},{10... | collective-permute-start | bytes 2985992 | tf_op jit(solution)/shard_map/ppermute | solution.py:26
  419.4 59.8 %collective-permute-start.32 = (bf16[1024,1152]{1,0:T(8,128)(2,1)S(1)}, bf16[1024,1152]{1,0:T(8,128)(2,1)S(1)}, u32[]{:S(2)}, u32[]{:S(2)}) collective-permute-start(bf16[1024,1152]{1,0:T(8,128)(2,1)S(1)} %add_convert_fusion), channel_id=1, source_target_pairs={{0,1},{1,0},{2,3},{3,2},{4,5},{5,4},{6,7},{7,6},{8,9},{9,8},{10,11... | collective-permute-start | bytes 7077896 | tf_op jit(solution)/shard_map/ppermute | solution.py:26
  435.0 104.8 %collective-permute-start.62 = (bf16[288,3456]{1,0:T(8,128)(2,1)}, bf16[288,3456]{1,0:T(8,128)(2,1)}, u32[]{:S(2)}, u32[]{:S(2)}) collective-permute-start(bf16[288,3456]{1,0:T(8,128)(2,1)} %pad_maximum_fusion.4), channel_id=1, source_target_pairs={{0,16},{8,24},{16,0},{24,8},{1,17},{9,25},{17,1},{25,9},{2,18},{10... | collective-permute-start | bytes 5971976 | tf_op jit(solution)/shard_map/ppermute | solution.py:26
  437.9 102.4 %collective-permute-start.60 = (bf16[288,3456]{1,0:T(8,128)(2,1)}, bf16[288,3456]{1,0:T(8,128)(2,1)}, u32[]{:S(2)}, u32[]{:S(2)}) collective-permute-start(bf16[288,3456]{1,0:T(8,128)(2,1)} %pad_maximum_fusion.3), channel_id=1, source_target_pairs={{0,8},{8,0},{16,24},{24,16},{1,9},{9,1},{17,25},{25,17},{2,10},{10... | collective-permute-start | bytes 5971976 | tf_op jit(solution)/shard_map/ppermute | solution.py:26
  477.6 117.2 %collective-permute-start.46 = (bf16[288,3456]{1,0:T(8,128)(2,1)}, bf16[288,3456]{1,0:T(8,128)(2,1)}, u32[]{:S(2)}, u32[]{:S(2)}) collective-permute-start(bf16[288,3456]{1,0:T(8,128)(2,1)} %pad_maximum_fusion.2), channel_id=1, source_target_pairs={{0,16},{8,24},{16,0},{24,8},{1,17},{9,25},{17,1},{25,9},{2,18},{10... | collective-permute-start | bytes 5971976 | tf_op jit(solution)/shard_map/ppermute | solution.py:26
  508.1 87.6 %collective-permute-start.44 = (bf16[288,3456]{1,0:T(8,128)(2,1)}, bf16[288,3456]{1,0:T(8,128)(2,1)}, u32[]{:S(2)}, u32[]{:S(2)}) collective-permute-start(bf16[288,3456]{1,0:T(8,128)(2,1)} %pad_maximum_fusion.1), channel_id=1, source_target_pairs={{0,8},{8,0},{16,24},{24,16},{1,9},{9,1},{17,25},{25,17},{2,10},{10... | collective-permute-start | bytes 5971976 | tf_op jit(solution)/shard_map/ppermute | solution.py:26
  535.5 55.3 %collective-permute-start.36 = (bf16[144,1536]{1,0:T(8,128)(2,1)}, bf16[144,1536]{1,0:T(8,128)(2,1)}, u32[]{:S(2)}, u32[]{:S(2)}) collective-permute-start(bf16[144,1536]{1,0:T(8,128)(2,1)} %get-tuple-element.113), channel_id=1, source_target_pairs={{0,16},{8,24},{16,0},{24,8},{1,17},{9,25},{17,1},{25,9},{2,18},{10... | collective-permute-start | bytes 1327112 | tf_op jit(solution)/shard_map/ppermute | solution.py:26
  545.1 87.5 %collective-permute-start.63 = (bf16[288,3456]{1,0:T(8,128)(2,1)}, bf16[288,3456]{1,0:T(8,128)(2,1)}, u32[]{:S(2)}, u32[]{:S(2)}) collective-permute-start(bf16[288,3456]{1,0:T(8,128)(2,1)} %add_convert_fusion.2), channel_id=1, source_target_pairs={{0,2},{6,4},{1,3},{7,5},{8,10},{14,12},{9,11},{15,13},{16,18},{22,... | collective-permute-start | bytes 5971976 | tf_op jit(solution)/shard_map/ppermute | solution.py:156
  648.4 112.6 %collective-permute-start.64 = (bf16[288,3456]{1,0:T(8,128)(2,1)S(1)}, bf16[288,3456]{1,0:T(8,128)(2,1)S(1)}, u32[]{:S(2)}, u32[]{:S(2)}) collective-permute-start(bf16[288,3456]{1,0:T(8,128)(2,1)S(1)} %add.594), channel_id=1, source_target_pairs={{2,4},{4,2},{3,5},{5,3},{10,12},{12,10},{11,13},{13,11},{18,20},{2... | collective-permute-start | bytes 5971976 | tf_op jit(solution)/shard_map/ppermute | solution.py:158
  665.9 98.2 %collective-permute-start.48 = (bf16[288,3456]{1,0:T(8,128)(2,1)S(1)}, bf16[288,3456]{1,0:T(8,128)(2,1)S(1)}, u32[]{:S(2)}, u32[]{:S(2)}) collective-permute-start(bf16[288,3456]{1,0:T(8,128)(2,1)S(1)} %add.582), channel_id=1, source_target_pairs={{2,4},{4,2},{3,5},{5,3},{10,12},{12,10},{11,13},{13,11},{18,20},{2... | collective-permute-start | bytes 5971976 | tf_op jit(solution)/shard_map/ppermute | solution.py:158
  668.1 97.8 %collective-permute-start.41 = (bf16[288,1536]{1,0:T(8,128)(2,1)S(1)}, bf16[288,1536]{1,0:T(8,128)(2,1)S(1)}, u32[]{:S(2)}, u32[]{:S(2)}) collective-permute-start(bf16[288,1536]{1,0:T(8,128)(2,1)S(1)} %add.576), channel_id=1, source_target_pairs={{2,4},{4,2},{3,5},{5,3},{10,12},{12,10},{11,13},{13,11},{18,20},{2... | collective-permute-start | bytes 2654216 | tf_op jit(solution)/shard_map/ppermute | solution.py:158
  671.4 88.3 %collective-permute-start.71 = (f32[1,1280]{1,0:T(1,128)S(1)}, f32[1,1280]{1,0:T(1,128)S(1)}, u32[]{:S(2)}, u32[]{:S(2)}) collective-permute-start(f32[1,1280]{1,0:T(1,128)S(1)} %fusion.129), channel_id=1, source_target_pairs={{0,4},{2,6},{4,0},{6,2},{1,5},{3,7},{5,1},{7,3},{8,12},{10,14},{12... | collective-permute-start | bytes 15368 | tf_op jit(solution)/shard_map/ppermute | solution.py:26
  677.1 82.6 %collective-permute-start.70 = (f32[1,1280]{1,0:T(1,128)S(1)}, f32[1,1280]{1,0:T(1,128)S(1)}, u32[]{:S(2)}, u32[]{:S(2)}) collective-permute-start(f32[1,1280]{1,0:T(1,128)S(1)} %fusion.129), channel_id=1, source_target_pairs={{0,2},{2,0},{4,6},{6,4},{1,3},{3,1},{5,7},{7,5},{8,10},{10,8},{12,... | collective-permute-start | bytes 15368 | tf_op jit(solution)/shard_map/ppermute | solution.py:26
  762.8 117.1 %collective-permute-start.65 = (bf16[288,3456]{1,0:T(8,128)(2,1)}, bf16[288,3456]{1,0:T(8,128)(2,1)}, u32[]{:S(2)}, u32[]{:S(2)}) collective-permute-start(bf16[288,3456]{1,0:T(8,128)(2,1)} %add.595), channel_id=1, source_target_pairs={{2,0},{4,6},{3,1},{5,7},{10,8},{12,14},{11,9},{13,15},{18,16},{20,... | collective-permute-start | bytes 5971976 | tf_op jit(solution)/shard_map/ppermute | solution.py:160
  764.6 122.0 %collective-permute-start.49 = (bf16[288,3456]{1,0:T(8,128)(2,1)S(1)}, bf16[288,3456]{1,0:T(8,128)(2,1)}, u32[]{:S(2)}, u32[]{:S(2)}) collective-permute-start(bf16[288,3456]{1,0:T(8,128)(2,1)S(1)} %add.583), channel_id=1, source_target_pairs={{2,0},{4,6},{3,1},{5,7},{10,8},{12,14},{11,9},{13,15},{18,16},{20,... | collective-permute-start | bytes 5971976 | tf_op jit(solution)/shard_map/ppermute | solution.py:160
  766.1 101.8 %collective-permute-start.42 = (bf16[288,1536]{1,0:T(8,128)(2,1)S(1)}, bf16[288,1536]{1,0:T(8,128)(2,1)}, u32[]{:S(2)}, u32[]{:S(2)}) collective-permute-start(bf16[288,1536]{1,0:T(8,128)(2,1)S(1)} %add.577), channel_id=1, source_target_pairs={{2,0},{4,6},{3,1},{5,7},{10,8},{12,14},{11,9},{13,15},{18,16},{20,... | collective-permute-start | bytes 2654216 | tf_op jit(solution)/shard_map/ppermute | solution.py:160
  769.1 102.7 %collective-permute-start.50 = (bf16[96,3456]{1,0:T(8,128)(2,1)S(1)}, bf16[96,3456]{1,0:T(8,128)(2,1)S(1)}, u32[]{:S(2)}, u32[]{:S(2)}) collective-permute-start(bf16[96,3456]{1,0:T(8,128)(2,1)S(1)} %get-tuple-element.128), channel_id=1, source_target_pairs={{0,2},{6,4},{1,3},{7,5},{8,10},{14,12},{9,11},{15,13},{16,18},{22,... | collective-permute-start | bytes 1990664 | tf_op jit(solution)/shard_map/ppermute | solution.py:156
  777.3 94.5 %collective-permute-start.56 = (bf16[96,3456]{1,0:T(8,128)(2,1)S(1)}, bf16[96,3456]{1,0:T(8,128)(2,1)S(1)}, u32[]{:S(2)}, u32[]{:S(2)}) collective-permute-start(bf16[96,3456]{1,0:T(8,128)(2,1)S(1)} %get-tuple-element.129), channel_id=1, source_target_pairs={{0,2},{6,4},{1,3},{7,5},{8,10},{14,12},{9,11},{15,13},{16,18},{22,... | collective-permute-start | bytes 1990664 | tf_op jit(solution)/shard_map/ppermute | solution.py:156
  (161 other events, 3797.8 us)
Sparse Core Ops, SparseCore 0:
  385.2 146.1 reduce-scatter.1

commit v2 on v1

--- a/solution.py
+++ b/solution.py
@@ -139,8 +139,8 @@
         return lax.dynamic_slice_in_dim(parts, me ^ flip, 1, 0)
 
     mine = part(0)
-    for flip in (1, 2, 3):
-        mine = mine + hop(part(flip), "fsdp", flip)
+    near, side, far = (hop(part(flip), "fsdp", flip) for flip in (1, 2, 3))
+    mine = ((mine + near) + side) + far
     one, two, three = (hop(mine, "ctx", flip) for flip in (1, 2, 3))
     return ((mine + one) + (two + three))[0]
 
@@ -369,9 +369,7 @@
         query_block, key_block, value_block, scores = block_of(index)
         weights = jnp.exp(scores - logsums[index])
         upper_grad = attended_heads[index * block_rows : (index + 1) * block_rows]
-        weight_grad = jnp.einsum(
-            "rhd,sd->hrs", upper_grad, value_block, preferred_element_type=F32
-        )
+        weight_grad = jnp.einsum("rhd,sd->hrs", upper_grad, value_block, preferred_element_type=F32)
         centred = jnp.sum(weights * weight_grad, axis=-1, keepdims=True)
         score_grad = (weights * (weight_grad - centred)).astype(BF16)
         query_parts[index] = (
@@ -393,7 +391,8 @@
         else:
             rows = rows + returned.astype(F32)
         own_grads.append(rows)
-    keyvalue_grad = summed_tp(jnp.concatenate(own_grads, axis=0).astype(BF16))
+    own_grads = jnp.concatenate(own_grads, axis=0).astype(BF16)
+    keyvalue_grad = summed_tp(own_grads)
 
     query_turned = jnp.concatenate(query_parts, axis=0)
     query_unturned = rotate(query_turned, cosine_heads, -sine_heads)
@@ -420,12 +419,14 @@
         residual_grad + norm_back(hidden_grad * input_factor, normed_in, inverse_in)
     ).astype(BF16)
 
-    down_share = reduced(down_grad, True, 1).T
-    gate_share = reduced(gate_weight_grad, True, 1)
-    up_share = reduced(up_weight_grad, False, 3)
-    attention_shares = reduced(
-        jnp.concatenate([qkv_weight_grad, output_weight_grad], axis=1), True, 1
-    )
+    down_share = reduced(down_grad, True, 2).T
+    gate_share = reduced(gate_weight_grad, False, 1)
+    attention_part = scatter_rows(
+        jnp.concatenate([qkv_weight_grad, output_weight_grad], axis=1), True
+    )
+    attention_shares = summed_ctx(attention_part, 1).astype(F32)
+    up_share = tied(scatter_rows(up_weight_grad, False), attention_part)
+    up_share = summed_ctx(up_share, 3).astype(F32)
     query_gain_grad = summed_tp(query_gain_part)
     gain_shares = summed_gains(
         jnp.concatenate(

time: 959 us -> 930 us (0.970)
  starting transfers between devices: 177 us -> 98.9 us
  local copies, waits for them, and re-layouts: 109 us -> 143 us
  other arithmetic: 116 us -> 135 us
    ppermute x53 -> x49, starting transfers between devices: 137 us -> 50 us  [hop(): lax.ppermute(value, axis, [(i, i ^ flip) for i in range(lax.axis_size(axi...]
    ppermute x6 -> x7, waiting for transfers between devices: 136 us -> 97.7 us  [summed_ctx(): outward = lax.ppermute(total, 'ctx', [(1, 0), (2, 3)])]
    ppermute x53 -> x49, waiting for transfers between devices: 186 us -> 210 us  [hop(): lax.ppermute(value, axis, [(i, i ^ flip) for i in range(lax.axis_size(axi...]
    ppermute x0 -> x7, local copies, waits for them, and re-layouts: none -> 14.4 us  [the longest x4 8.99 us: hop(): lax.ppermute(value, axis, [(i, i ^ flip) for i in range(lax.axis_size(axi...]
    add x6 -> x7, other arithmetic: 2.93 us -> 13.2 us  [summed_ctx(): total = pair + across]
    ppermute x6 -> x7, waiting for transfers between devices: 33.3 us -> 42.6 us  [summed_ctx(): inward = lax.ppermute(part, 'ctx', [(0, 1), (3, 2)])]
    ppermute x6 -> x7, starting transfers between devices: 21.8 us -> 22.4 us  [summed_ctx(): inward = lax.ppermute(part, 'ctx', [(0, 1), (3, 2)])]
    unnamed x223 -> x216, local copies, waits for them, and re-layouts: 23.5 us -> 23.1 us
  transfers between devices with their start and end apart: 74 -> 74, of which waited for: 30 -> 30; matrix products, arithmetic and copies ran while one was open for 29% -> 37% of each run, Pallas kernels for 0% -> 0%
where the time goes in v2:
time: 930 us; the launch traced here: 920 us
  waiting for transfers between devices  352 us (38%)
  matrix products  175 us (19%)
  local copies, waits for them, and re-layouts  143 us (15%)
  other arithmetic  135 us (15%)
  starting transfers between devices  98.9 us (11%)
  between operations  16.2 us (2%)
    ppermute x49, waiting for transfers between devices, hop(): lax.ppermute(value, axis, [(i, i ^ flip) for i in range(lax.axis_size(axi...  210 us
    ppermute x7, waiting for transfers between devices, summed_ctx(): outward = lax.ppermute(total, 'ctx', [(1, 0), (2, 3)])  97.7 us
    dot_general x5, matrix products, product(): return jnp.dot(left, right, preferred_element_type=F32)  59.8 us
    dot_general x6, matrix products, inner_cols(): lax.dot_general(left, right, (((1,), (1,)), ((), ())), preferred_element_...  55.6 us
    ppermute x49, starting transfers between devices, hop(): lax.ppermute(value, axis, [(i, i ^ flip) for i in range(lax.axis_size(axi...  50 us
    dot_general x5, matrix products, inner_rows(): lax.dot_general(left, right, (((0,), (0,)), ((), ())), preferred_element_...  43.1 us
    ppermute x7, waiting for transfers between devices, summed_ctx(): inward = lax.ppermute(part, 'ctx', [(0, 1), (3, 2)])  42.6 us
    dynamic_update_slice x41, local copies, waits for them, and re-layouts, put_rows(): return lax.dynamic_update_slice_in_dim(full, rows, start, 0)  34.1 us
  transfers between devices with their start and end apart: 74, of which 30 were waited for; matrix products, arithmetic and copies ran while one was open for 37% of the time, Pallas kernels for 0%

profile of v2, /device:TPU:0, one launch (start us, length us, event | category | flops | bytes accessed | tf_op | source)
XLA Modules:
  0.0 919.7 jit_solution(1562536529349667609)
XLA Ops:
  113.8 33.7 %collective-permute-done.16 = bf16[96,3456]{1,0:T(8,128)(2,1)S(1)} collective-permute-done((bf16[96,3456]{1,0:T(8,128)(2,1)S(1)}, bf16[96,3456]{1,0:T(8,128)(2,1)S(1)}, u32[]{:S(2)}, u32[]{:S(2)}) %collective-permute-start.16) | collective-permute-done | bytes 663584 | tf_op jit(solution)/shard_map/ppermute | solution.py:26
  153.8 25.6 %collective-permute-done.15 = bf16[192,3456]{1,0:T(8,128)(2,1)S(1)} collective-permute-done((bf16[192,3456]{1,0:T(8,128)(2,1)S(1)}, bf16[192,3456]{1,0:T(8,128)(2,1)S(1)}, u32[]{:S(2)}, u32[]{:S(2)}) %collective-permute-start.15) | collective-permute-done | bytes 1327136 | tf_op jit(solution)/shard_map/ppermute | solution.py:26
  205.9 12.3 %fusion.154 = f32[1024,3456]{1,0:T(8,128)} fusion(bf16[1024,1152]{1,0:T(8,128)(2,1)S(1)} %multiply_convert_fusion.3, bf16[1152,3456]{1,0:T(8,128)(2,1)S(1)} %constant_dynamic-update-slice_fusion.14), kind=kOutput, calls=%fused_computation.359 | convolution fusion | flops 8153726976 | bytes 24477696 | tf_op jit(solution)/shard_map/dot_general | solution.py:199
  247.6 19.7 %multiply_convert_fusion.1 = (bf16[1024,3456]{1,0:T(8,128)(2,1)}, f32[1024,3456]{1,0:T(8,128)}) fusion(f32[1024,3456]{1,0:T(8,128)} %fusion.154, bf16[1024,1152]{1,0:T(8,128)(2,1)} %copy-done.38, bf16[1152,3456]{1,0:T(8,128)(2,1)} %constant_dynamic-update-slice_fusion.7), kind=kOutput, calls=%fused_computation.13 | convolution fusion | flops 8189116416 | bytes 45711360 | tf_op jit(solution)/shard_map/dot_general | solution.py:199
  290.0 11.1 %convolution_convert_fusion.3 = bf16[1024,1152]{1,0:T(8,128)(2,1)} fusion(bf16[1024,3456]{1,0:T(8,128)(2,1)S(1)} %copy-done.96, bf16[1152,3456]{1,0:T(8,128)(2,1)S(1)} %constant_dynamic-update-slice_fusion), kind=kOutput, calls=%fused_computation.91 | convolution fusion | flops 8154906624 | bytes 17399808 | tf_op jit(solution)/shard_map/dot_general | solution.py:207
  320.0 11.0 %convolution_convert_fusion.2 = bf16[1152,3456]{1,0:T(8,128)(2,1)} fusion(bf16[1024,1152]{1,0:T(8,128)(2,1)S(1)} %get-tuple-element.29, bf16[1024,3456]{1,0:T(8,128)(2,1)S(1)} %bitcast.165), kind=kOutput, calls=%fused_computation.4 | convolution fusion | flops 8157708288 | bytes 17399808 | tf_op jit(solution)/shard_map/dot_general | solution.py:203
  331.0 21.5 %multiply_convert_fusion = (bf16[1024,3456]{1,0:T(8,128)(2,1)}, bf16[1024,3456]{1,0:T(8,128)(2,1)}) fusion(f32[1024,3456]{1,0:T(8,128)} %fusion.154, f32[1024,3456]{1,0:T(8,128)} %get-tuple-element.180, bf16[1024,1152]{1,0:T(8,128)(2,1)S(1)} %get-tuple-element.29, bf16[1152,3456]{1,0:T(8,128)(2,1)S(1)} %bitcast.149), kind=kOutput, calls=%fused_computation.12 | convolution fusion | flops 8238661632 | bytes 52789248 | tf_op jit(solution)/shard_map/dot_general | solution.py:199
  352.6 13.7 %convolution_convert_fusion.1 = bf16[1152,3456]{1,0:T(8,128)(2,1)} fusion(bf16[1024,1152]{1,0:T(8,128)(2,1)} %copy-done.38, bf16[1024,3456]{1,0:T(8,128)(2,1)} %get-tuple-element.31), kind=kOutput, calls=%fused_computation.3 | convolution fusion | flops 8157708288 | bytes 17399808 | tf_op jit(solution)/shard_map/dot_general | solution.py:203
  366.3 13.8 %convolution_convert_fusion = bf16[1152,3456]{1,0:T(8,128)(2,1)} fusion(bf16[1024,1152]{1,0:T(8,128)(2,1)} %copy-done.38, bf16[1024,3456]{1,0:T(8,128)(2,1)} %get-tuple-element.32), kind=kOutput, calls=%fused_computation.2 | convolution fusion | flops 8157708288 | bytes 17399808 | tf_op jit(solution)/shard_map/dot_general | solution.py:203
  387.4 16.2 %fusion.155 = f32[1024,1152]{1,0:T(8,128)} fusion(bf16[1024,3456]{1,0:T(8,128)(2,1)} %get-tuple-element.32, bf16[1152,3456]{1,0:T(8,128)(2,1)} %constant_dynamic-update-slice_fusion.7), kind=kOutput, calls=%fused_computation.360 | convolution fusion | flops 8153726976 | bytes 19759104 | tf_op jit(solution)/shard_map/dot_general | solution.py:207
  403.6 13.6 %add_convert_fusion = bf16[1024,1152]{1,0:T(8,128)(2,1)} fusion(f32[1024,1152]{1,0:T(8,128)} %fusion.155, bf16[1024,3456]{1,0:T(8,128)(2,1)} %get-tuple-element.31, bf16[1152,3456]{1,0:T(8,128)(2,1)S(1)} %bitcast.151), kind=kOutput, calls=%fused_computation.53 | convolution fusion | flops 8156086272 | bytes 22118400 | tf_op jit(solution)/shard_map/dot_general | solution.py:207
  417.3 14.0 %collective-permute-done.57 = bf16[144,3456]{1,0:T(8,128)(2,1)} collective-permute-done((bf16[144,3456]{1,0:T(8,128)(2,1)}, bf16[144,3456]{1,0:T(8,128)(2,1)}, u32[]{:S(2)}, u32[]{:S(2)}) %collective-permute-start.57) | collective-permute-done | bytes 995360 | tf_op jit(solution)/shard_map/ppermute | solution.py:26
  471.8 41.1 %collective-permute-done.58 = bf16[288,3456]{1,0:T(8,128)(2,1)S(1)} collective-permute-done((bf16[288,3456]{1,0:T(8,128)(2,1)S(1)}, bf16[288,3456]{1,0:T(8,128)(2,1)S(1)}, u32[]{:S(2)}, u32[]{:S(2)}) %collective-permute-start.58) | collective-permute-done | bytes 1990688 | tf_op jit(solution)/shard_map/ppermute | solution.py:26
  554.8 7.5 collective-permute-done.62
  616.1 13.9 %collective-permute-done.37 = bf16[288,1536]{1,0:T(8,128)(2,1)} collective-permute-done((bf16[288,1536]{1,0:T(8,128)(2,1)}, bf16[288,1536]{1,0:T(8,128)(2,1)}, u32[]{:S(2)}, u32[]{:S(2)}) %collective-permute-start.37) | collective-permute-done | bytes 884768 | tf_op jit(solution)/shard_map/ppermute | solution.py:26
  647.8 12.3 %collective-permute-done.40 = bf16[288,1536]{1,0:T(8,128)(2,1)S(1)} collective-permute-done((bf16[288,1536]{1,0:T(8,128)(2,1)}, bf16[288,1536]{1,0:T(8,128)(2,1)S(1)}, u32[]{:S(2)}, u32[]{:S(2)}) %collective-permute-start.40) | collective-permute-done | bytes 884768 | tf_op jit(solution)/shard_map/ppermute | solution.py:156
  666.6 8.5 fusion.22
  686.4 6.9 collective-permute-start.46
  711.3 10.9 %collective-permute-done.52 = bf16[96,3456]{1,0:T(8,128)(2,1)} collective-permute-done((bf16[96,3456]{1,0:T(8,128)(2,1)}, bf16[96,3456]{1,0:T(8,128)(2,1)}, u32[]{:S(2)}, u32[]{:S(2)}) %collective-permute-start.52) | collective-permute-done | bytes 663584 | tf_op jit(solution)/shard_map/ppermute | solution.py:156
  724.7 11.7 %collective-permute-done.49 = bf16[96,3456]{1,0:T(8,128)(2,1)} collective-permute-done((bf16[96,3456]{1,0:T(8,128)(2,1)}, bf16[96,3456]{1,0:T(8,128)(2,1)}, u32[]{:S(2)}, u32[]{:S(2)}) %collective-permute-start.49) | collective-permute-done | bytes 663584 | tf_op jit(solution)/shard_map/ppermute | solution.py:156
  741.2 35.7 %collective-permute-done.71 = f32[1,1280]{1,0:T(1,128)S(1)} collective-permute-done((f32[1,1280]{1,0:T(1,128)S(1)}, f32[1,1280]{1,0:T(1,128)S(1)}, u32[]{:S(2)}, u32[]{:S(2)}) %collective-permute-start.71) | collective-permute-done | bytes 5152 | tf_op jit(solution)/shard_map/ppermute | solution.py:26
  810.9 46.0 %collective-permute-done.51 = bf16[96,3456]{1,0:T(8,128)(2,1)S(1)} collective-permute-done((bf16[96,3456]{1,0:T(8,128)(2,1)S(1)}, bf16[96,3456]{1,0:T(8,128)(2,1)S(1)}, u32[]{:S(2)}, u32[]{:S(2)}) %collective-permute-start.51) | collective-permute-done | bytes 663584 | tf_op jit(solution)/shard_map/ppermute | solution.py:160
  857.0 14.1 %collective-permute-done.54 = bf16[96,3456]{1,0:T(8,128)(2,1)S(1)} collective-permute-done((bf16[96,3456]{1,0:T(8,128)(2,1)S(1)}, bf16[96,3456]{1,0:T(8,128)(2,1)S(1)}, u32[]{:S(2)}, u32[]{:S(2)}) %collective-permute-start.54) | collective-permute-done | bytes 663584 | tf_op jit(solution)/shard_map/ppermute | solution.py:160
  873.4 37.0 %collective-permute-done.45 = bf16[288,3456]{1,0:T(8,128)(2,1)S(1)} collective-permute-done((bf16[288,3456]{1,0:T(8,128)(2,1)S(1)}, bf16[288,3456]{1,0:T(8,128)(2,1)S(1)}, u32[]{:S(2)}, u32[]{:S(2)}) %collective-permute-start.45) | collective-permute-done | bytes 1990688 | tf_op jit(solution)/shard_map/ppermute | solution.py:160
  (576 shorter events, 451.4 us)
Async XLA Ops:
  7.2 676.4 %reduce-scatter.5.cloned.1.call-start = ((), (), s32[]{:S(2)}) async-start(), calls=%async_computation.3 | async-start | bytes 9953280 | tf_op jit(solution)/shard_map/reduce_scatter | solution.py:113
  47.0 54.4 %collective-permute-start.14 = (bf16[192,3456]{1,0:T(8,128)(2,1)}, bf16[192,3456]{1,0:T(8,128)(2,1)}, u32[]{:S(2)}, u32[]{:S(2)}) collective-permute-start(bf16[192,3456]{1,0:T(8,128)(2,1)} %pad_maximum_fusion.3), channel_id=1, source_target_pairs={{0,16},{8,24},{16,0},{24,8},{1,17},{9,25},{17,1},{25,9},{2,18},{10... | collective-permute-start | bytes 3981320 | tf_op jit(solution)/shard_map/ppermute | solution.py:26
  48.9 52.5 %collective-permute-start.13 = (bf16[192,3456]{1,0:T(8,128)(2,1)}, bf16[192,3456]{1,0:T(8,128)(2,1)}, u32[]{:S(2)}, u32[]{:S(2)}) collective-permute-start(bf16[192,3456]{1,0:T(8,128)(2,1)} %pad_maximum_fusion.3), channel_id=1, source_target_pairs={{0,8},{8,0},{16,24},{24,16},{1,9},{9,1},{17,25},{25,17},{2,10},{10... | collective-permute-start | bytes 3981320 | tf_op jit(solution)/shard_map/ppermute | solution.py:26
  101.3 98.0 %collective-permute-start.12 = (bf16[1024,1152]{1,0:T(8,128)(2,1)S(1)}, bf16[1024,1152]{1,0:T(8,128)(2,1)S(1)}, u32[]{:S(2)}, u32[]{:S(2)}) collective-permute-start(bf16[1024,1152]{1,0:T(8,128)(2,1)S(1)} %convolution_convert_fusion.5), channel_id=1, source_target_pairs={{0,1},{1,0},{2,3},{3,2},{4,5},{5,4},{6,7},{7,6},{8,9},{9,8},{10,11... | collective-permute-start | bytes 7077896 | tf_op jit(solution)/shard_map/ppermute | solution.py:26
  101.8 46.5 %collective-permute-start.20 = (bf16[192,3456]{1,0:T(8,128)(2,1)S(1)}, bf16[192,3456]{1,0:T(8,128)(2,1)S(1)}, u32[]{:S(2)}, u32[]{:S(2)}) collective-permute-start(bf16[192,3456]{1,0:T(8,128)(2,1)S(1)} %pad_maximum_fusion.5), channel_id=1, source_target_pairs={{0,16},{8,24},{16,0},{24,8},{1,17},{9,25},{17,1},{25,9},{2,18},{10... | collective-permute-start | bytes 3981320 | tf_op jit(solution)/shard_map/ppermute | solution.py:26
  102.0 47.6 %collective-permute-start.19 = (bf16[192,3456]{1,0:T(8,128)(2,1)S(1)}, bf16[192,3456]{1,0:T(8,128)(2,1)S(1)}, u32[]{:S(2)}, u32[]{:S(2)}) collective-permute-start(bf16[192,3456]{1,0:T(8,128)(2,1)S(1)} %pad_maximum_fusion.5), channel_id=1, source_target_pairs={{0,8},{8,0},{16,24},{24,16},{1,9},{9,1},{17,25},{25,17},{2,10},{10... | collective-permute-start | bytes 3981320 | tf_op jit(solution)/shard_map/ppermute | solution.py:26
  106.8 86.4 %collective-permute-start.18 = (bf16[96,3456]{1,0:T(8,128)(2,1)S(1)}, bf16[96,3456]{1,0:T(8,128)(2,1)S(1)}, u32[]{:S(2)}, u32[]{:S(2)}) collective-permute-start(bf16[96,3456]{1,0:T(8,128)(2,1)S(1)} %get-tuple-element.143), channel_id=1, source_target_pairs={{0,16},{8,24},{16,0},{24,8},{1,17},{9,25},{17,1},{25,9},{2,18},{10... | collective-permute-start | bytes 1990664 | tf_op jit(solution)/shard_map/ppermute | solution.py:26
  151.0 72.0 %collective-permute-start.26 = (bf16[192,3456]{1,0:T(8,128)(2,1)}, bf16[192,3456]{1,0:T(8,128)(2,1)}, u32[]{:S(2)}, u32[]{:S(2)}) collective-permute-start(bf16[192,3456]{1,0:T(8,128)(2,1)} %pad_maximum_fusion.7), channel_id=1, source_target_pairs={{0,16},{8,24},{16,0},{24,8},{1,17},{9,25},{17,1},{25,9},{2,18},{10... | collective-permute-start | bytes 3981320 | tf_op jit(solution)/shard_map/ppermute | solution.py:26
  179.5 46.2 %collective-permute-start.25 = (bf16[192,3456]{1,0:T(8,128)(2,1)}, bf16[192,3456]{1,0:T(8,128)(2,1)}, u32[]{:S(2)}, u32[]{:S(2)}) collective-permute-start(bf16[192,3456]{1,0:T(8,128)(2,1)} %pad_maximum_fusion.7), channel_id=1, source_target_pairs={{0,8},{8,0},{16,24},{24,16},{1,9},{9,1},{17,25},{25,17},{2,10},{10... | collective-permute-start | bytes 3981320 | tf_op jit(solution)/shard_map/ppermute | solution.py:26
  193.2 53.5 %collective-permute-start.24 = (bf16[96,3456]{1,0:T(8,128)(2,1)}, bf16[96,3456]{1,0:T(8,128)(2,1)S(1)}, u32[]{:S(2)}, u32[]{:S(2)}) collective-permute-start(bf16[96,3456]{1,0:T(8,128)(2,1)} %get-tuple-element.146), channel_id=1, source_target_pairs={{0,16},{8,24},{16,0},{24,8},{1,17},{9,25},{17,1},{25,9},{2,18},{10... | collective-permute-start | bytes 1990664 | tf_op jit(solution)/shard_map/ppermute | solution.py:26
  228.0 57.6 %collective-permute-start.30 = (bf16[96,3456]{1,0:T(8,128)(2,1)}, bf16[96,3456]{1,0:T(8,128)(2,1)}, u32[]{:S(2)}, u32[]{:S(2)}) collective-permute-start(bf16[96,3456]{1,0:T(8,128)(2,1)} %get-tuple-element.140), channel_id=1, source_target_pairs={{0,16},{8,24},{16,0},{24,8},{1,17},{9,25},{17,1},{25,9},{2,18},{10... | collective-permute-start | bytes 1990664 | tf_op jit(solution)/shard_map/ppermute | solution.py:26
  380.1 317.5 %reduce-scatter.3.cloned.1.call-start = ((), (), s32[]{:S(2)}) async-start(), calls=%async_computation.2 | async-start | bytes 9953280 | tf_op jit(solution)/shard_map/reduce_scatter | solution.py:113
  435.6 77.2 %collective-permute-start.58 = (bf16[288,3456]{1,0:T(8,128)(2,1)S(1)}, bf16[288,3456]{1,0:T(8,128)(2,1)S(1)}, u32[]{:S(2)}, u32[]{:S(2)}) collective-permute-start(bf16[288,3456]{1,0:T(8,128)(2,1)S(1)} %pad_maximum_fusion.2), channel_id=1, source_target_pairs={{0,16},{8,24},{16,0},{24,8},{1,17},{9,25},{17,1},{25,9},{2,18},{10... | collective-permute-start | bytes 5971976 | tf_op jit(solution)/shard_map/ppermute | solution.py:26
  436.8 76.2 %collective-permute-start.56 = (bf16[288,3456]{1,0:T(8,128)(2,1)S(1)}, bf16[288,3456]{1,0:T(8,128)(2,1)}, u32[]{:S(2)}, u32[]{:S(2)}) collective-permute-start(bf16[288,3456]{1,0:T(8,128)(2,1)S(1)} %pad_maximum_fusion.1), channel_id=1, source_target_pairs={{0,8},{8,0},{16,24},{24,16},{1,9},{9,1},{17,25},{25,17},{2,10},{10... | collective-permute-start | bytes 5971976 | tf_op jit(solution)/shard_map/ppermute | solution.py:26
  471.7 52.8 %collective-permute-start.35 = (bf16[1024,512]{0,1:T(8,128)(2,1)S(1)}, bf16[1024,512]{0,1:T(8,128)(2,1)S(1)}, u32[]{:S(2)}, u32[]{:S(2)}) collective-permute-start(bf16[1024,512]{0,1:T(8,128)(2,1)S(1)} %pad_maximum_fusion.16), channel_id=1, source_target_pairs={{0,1},{1,0},{2,3},{3,2},{4,5},{5,4},{6,7},{7,6},{8,9},{9,8},{10,11... | collective-permute-start | bytes 3145736 | tf_op jit(solution)/shard_map/ppermute | solution.py:26
  610.3 56.3 %collective-permute-start.33 = (bf16[1024,1152]{1,0:T(8,128)(2,1)}, bf16[1024,1152]{1,0:T(8,128)(2,1)}, u32[]{:S(2)}, u32[]{:S(2)}) collective-permute-start(bf16[1024,1152]{1,0:T(8,128)(2,1)} %convolution_convert_fusion.4), channel_id=1, source_target_pairs={{0,1},{1,0},{2,3},{3,2},{4,5},{5,4},{6,7},{7,6},{8,9},{9,8},{10,11... | collective-permute-start | bytes 7077896 | tf_op jit(solution)/shard_map/ppermute | solution.py:26
  697.6 80.8 %collective-permute-start.43 = (bf16[288,3456]{1,0:T(8,128)(2,1)}, bf16[288,3456]{1,0:T(8,128)(2,1)}, u32[]{:S(2)}, u32[]{:S(2)}) collective-permute-start(bf16[288,3456]{1,0:T(8,128)(2,1)} %reduce-scatter.3.cloned.1.call-done), channel_id=1, source_target_pairs={{0,2},{6,4},{1,3},{7,5},{8,10},{14,12},{9,11},{15,13},{16,18},{22,... | collective-permute-start | bytes 5971976 | tf_op jit(solution)/shard_map/ppermute | solution.py:156
  706.5 70.4 %collective-permute-start.71 = (f32[1,1280]{1,0:T(1,128)S(1)}, f32[1,1280]{1,0:T(1,128)S(1)}, u32[]{:S(2)}, u32[]{:S(2)}) collective-permute-start(f32[1,1280]{1,0:T(1,128)S(1)} %fusion.129), channel_id=1, source_target_pairs={{0,6},{2,4},{4,2},{6,0},{1,7},{3,5},{5,3},{7,1},{8,14},{10,12},{12... | collective-permute-start | bytes 15368 | tf_op jit(solution)/shard_map/ppermute | solution.py:26
  711.3 67.1 %collective-permute-start.70 = (f32[1,1280]{1,0:T(1,128)S(1)}, f32[1,1280]{1,0:T(1,128)S(1)}, u32[]{:S(2)}, u32[]{:S(2)}) collective-permute-start(f32[1,1280]{1,0:T(1,128)S(1)} %fusion.129), channel_id=1, source_target_pairs={{0,4},{2,6},{4,0},{6,2},{1,5},{3,7},{5,1},{7,3},{8,12},{10,14},{12... | collective-permute-start | bytes 15368 | tf_op jit(solution)/shard_map/ppermute | solution.py:26
  722.3 56.2 %collective-permute-start.69 = (f32[1,1280]{1,0:T(1,128)S(1)}, f32[1,1280]{1,0:T(1,128)S(1)}, u32[]{:S(2)}, u32[]{:S(2)}) collective-permute-start(f32[1,1280]{1,0:T(1,128)S(1)} %fusion.129), channel_id=1, source_target_pairs={{0,2},{2,0},{4,6},{6,4},{1,3},{3,1},{5,7},{7,5},{8,10},{10,8},{12,... | collective-permute-start | bytes 15368 | tf_op jit(solution)/shard_map/ppermute | solution.py:26
  736.5 47.2 %collective-permute-start.42 = (bf16[288,1536]{1,0:T(8,128)(2,1)}, bf16[288,1536]{1,0:T(8,128)(2,1)}, u32[]{:S(2)}, u32[]{:S(2)}) collective-permute-start(bf16[288,1536]{1,0:T(8,128)(2,1)} %copy.133), channel_id=1, source_target_pairs={{2,0},{4,6},{3,1},{5,7},{10,8},{12,14},{11,9},{13,15},{18,16},{20,... | collective-permute-start | bytes 2654216 | tf_op jit(solution)/shard_map/ppermute | solution.py:160
  802.3 54.6 %collective-permute-start.51 = (bf16[96,3456]{1,0:T(8,128)(2,1)S(1)}, bf16[96,3456]{1,0:T(8,128)(2,1)S(1)}, u32[]{:S(2)}, u32[]{:S(2)}) collective-permute-start(bf16[96,3456]{1,0:T(8,128)(2,1)S(1)} %add.569), channel_id=1, source_target_pairs={{2,0},{4,6},{3,1},{5,7},{10,8},{12,14},{11,9},{13,15},{18,16},{20,... | collective-permute-start | bytes 1990664 | tf_op jit(solution)/shard_map/ppermute | solution.py:160
  805.0 66.1 %collective-permute-start.54 = (bf16[96,3456]{1,0:T(8,128)(2,1)S(1)}, bf16[96,3456]{1,0:T(8,128)(2,1)S(1)}, u32[]{:S(2)}, u32[]{:S(2)}) collective-permute-start(bf16[96,3456]{1,0:T(8,128)(2,1)S(1)} %add.571), channel_id=1, source_target_pairs={{2,0},{4,6},{3,1},{5,7},{10,8},{12,14},{11,9},{13,15},{18,16},{20,... | collective-permute-start | bytes 1990664 | tf_op jit(solution)/shard_map/ppermute | solution.py:160
  809.6 100.8 %collective-permute-start.45 = (bf16[288,3456]{1,0:T(8,128)(2,1)S(1)}, bf16[288,3456]{1,0:T(8,128)(2,1)S(1)}, u32[]{:S(2)}, u32[]{:S(2)}) collective-permute-start(bf16[288,3456]{1,0:T(8,128)(2,1)S(1)} %add.565), channel_id=1, source_target_pairs={{2,0},{4,6},{3,1},{5,7},{10,8},{12,14},{11,9},{13,15},{18,16},{20,... | collective-permute-start | bytes 5971976 | tf_op jit(solution)/shard_map/ppermute | solution.py:160
  (156 other events, 2696.4 us)
Sparse Core Ops, SparseCore 0:
  380.2 136.9 reduce-scatter.4
  520.3 111.3 reduce-scatter.2
